TPU v7x, 512 devices: a whole 4x4x16 slice. The times are simulated.
512 devices in a mesh: pop: 16 (over z), tp: 32 (over y, x, core).
Axes of the slice: x: 4, y: 4, z: 16, core: 2. Of those that a mesh axis runs over, the one named last changes fastest.
Arguments:
- in_spikes: int32 [4, 15, 4096], replicated, may hold values 0 or 1
- w_in: bfloat16 [4096, 4096], P(None, 'tp'), may hold values from -0.1875 to 0.1875
- w_rec: bfloat16 [4096, 4096], P(None, 'tp'), may hold values from -0.1875 to 0.1875
- leak_rate: float32 [4096], P('tp'), may hold values from 0.5 to 0.95
- neuron_bias: float32 [4096], P('tp'), may hold values from -2.5 to 2.5
- readout: float32 [4096], P('tp'), may hold values from -0.1875 to 0.1875
- pert_table: bfloat16 [256, 4096], P(None, 'tp'), may hold values from -4 to 4
- pert_idx: int32 [512, 2], P('pop'), may hold values from 0 to 255
- member_ranks: int32 [512], P('pop'), may hold values from 0 to 511, each once
Outputs:
- returns: float32 [512], P('pop')
- grad_rec: bfloat16 [4096, 4096], P(None, 'tp')
Inputs may be any that keep to these rules, and one draw needn't show every extreme that they name: member_ranks holds each of 0 to 511 once.
All inputs are finite; a program needn't handle non-finite values.
Results may differ from a plain program's by a relative error of at most 0.0044.
Values may be sent and summed in bfloat16 or wider, within the bound.
A program may use at most 64 MiB of HBM per device.

v0:
```python
import jax
import jax.numpy as jnp
from jax import lax
from jax.sharding import PartitionSpec as P

sigma_scale = 0.01


def shards(
    in_spikes, w_in, w_rec, leak_rate, neuron_bias, readout, pert_table, pert_idx, member_ranks
):
    step_count, episodes, inputs = in_spikes.shape
    members_dev = pert_idx.shape[0]
    local_width = w_rec.shape[1]
    row_count = members_dev * episodes
    member_count = members_dev * lax.axis_size("pop")
    spike_input = in_spikes.astype(jnp.bfloat16).reshape(step_count * episodes, inputs)
    input_drive = jnp.dot(spike_input, w_in, preferred_element_type=jnp.float32) + neuron_bias
    input_drive = input_drive.reshape(step_count, episodes, local_width)
    post_side = jnp.take(pert_table, pert_idx[:, 1], axis=0).astype(jnp.float32)
    pre_local = jnp.take(pert_table, pert_idx[:, 0], axis=0)
    membrane = jnp.zeros((members_dev, episodes, local_width), jnp.float32)
    spikes = jnp.zeros((members_dev, episodes, local_width), jnp.bfloat16)
    readout_sum = jnp.zeros((members_dev, episodes), jnp.float32)
    for moment in range(step_count):
        current = input_drive[moment][None]
        if moment > 0:
            flat_spikes = spikes.reshape(row_count, local_width)
            recurrent = jnp.dot(
                lax.all_gather(flat_spikes, "tp", axis=1, tiled=True),
                w_rec,
                preferred_element_type=jnp.float32,
            )
            partial_proj = jnp.einsum(
                "men,mn->me", spikes, pre_local, preferred_element_type=jnp.float32
            )
            projection = lax.psum(partial_proj, "tp")
            current = (
                current
                + recurrent.reshape(members_dev, episodes, local_width)
                + sigma_scale * projection[:, :, None] * post_side[:, None, :]
            )
        membrane = leak_rate * (membrane - spikes.astype(jnp.float32)) + current
        spikes = jax.nn.sigmoid(4.0 * (membrane - 1.0)).astype(jnp.bfloat16)
        readout_sum = readout_sum + jnp.einsum(
            "men,n->me", spikes.astype(jnp.float32), readout, precision=lax.Precision.HIGHEST
        )
    returns = lax.psum(jnp.sum(readout_sum, axis=1), "tp") / (episodes * step_count)
    fitness = member_ranks.astype(jnp.float32) / (member_count - 1) - 0.5 + returns
    full_table = lax.all_gather(pert_table, "tp", axis=1, tiled=True)
    pre_side = jnp.take(full_table, pert_idx[:, 0], axis=0)
    weighted = pre_side.astype(jnp.float32) * fitness[:, None]
    partial_grad = jnp.dot(weighted.T, post_side, precision=lax.Precision.HIGHEST)
    grad_total = lax.psum(partial_grad, "pop")
    grad_rec = (grad_total * jnp.sqrt(12.0 / member_count)).astype(jnp.bfloat16)
    return (returns, grad_rec)


def solution(mesh):
    placed = (
        P(),
        P(None, "tp"),
        P(None, "tp"),
        P("tp"),
        P("tp"),
        P("tp"),
        P(None, "tp"),
        P("pop", None),
        P("pop"),
    )
    return jax.shard_map(
        shards, mesh=mesh, in_specs=placed, out_specs=(P("pop"), P(None, "tp")), check_vma=False
    )
```

profile of v0, /device:TPU:1, one launch (start us, length us, event | category | flops | bytes accessed | tf_op | source)
XLA Modules:
  0.0 620.0 jit_solution(11795909745084561978)
XLA Ops:
  7.2 0.0 all-gather.5.cloned.1.call-start
  7.3 1.5 convert_element_type.59
  8.7 0.3 copy.12
  9.0 0.2 reshape.59
  9.2 1.5 convolution_add_fusion
  10.8 0.7 divide_convert_fusion.5
  11.5 0.0 all-gather.5.cloned.1.call-update
  11.6 0.0 all-gather.7.cloned.1.call-start
  11.7 0.6 gather_fusion.2
  12.3 0.1 fusion.31
  12.4 0.6 gather_fusion.1
  13.0 0.1 select_bitcast_fusion
  13.1 0.2 fusion.23
  13.3 125.5 %psum.35 = f32[32,15]{1,0:T(8,128)S(1)} all-reduce(f32[32,15]{1,0:T(8,128)S(1)} %bitcast.55), channel_id=1, replica_groups=mesh['pop'=16,'tp'=32] {'tp'}, use_global_device_ids=true, to_apply=%region_0.0 | all-reduce | flops 480 | bytes 3840 | tf_op jit(solution)/shard_map/psum | solution.py:37
  138.8 0.1 mul.157
  139.0 0.0 all-gather.5.cloned.1.call-done
  139.0 4.0 divide_convert_fusion.4
  143.0 0.0 all-gather.7.cloned.1.call-update
  143.0 0.0 all-gather.11.cloned.1.call-start
  143.0 0.7 all-gather.11.cloned.1.call-update
  143.7 0.0 all-gather.9.cloned.1.call-start
  143.9 0.2 divide_convert_fusion.2
  144.1 0.2 fusion.27
  144.2 124.4 %psum.36 = f32[32,15]{1,0:T(8,128)S(1)} all-reduce(f32[32,15]{1,0:T(8,128)S(1)} %bitcast.56), channel_id=1, replica_groups=mesh['pop'=16,'tp'=32] {'tp'}, use_global_device_ids=true, to_apply=%region_1.3 | all-reduce | flops 480 | bytes 3840 | tf_op jit(solution)/shard_map/psum | solution.py:37
  268.6 0.1 mul.168
  268.7 0.0 all-gather.7.cloned.1.call-done
  268.8 4.0 divide_convert_fusion.3
  272.8 0.0 all-reduce.2.cloned.1.call-start
  272.9 0.7 all-gather.11.cloned.1.call-done
  273.6 2.8 gather_fusion
  276.4 0.2 fusion.19
  276.7 0.2 copy.18
  276.8 0.3 divide_convert_fusion.1
  277.1 0.2 fusion.17
  277.4 0.2 copy.21
  277.5 0.2 fusion.21
  277.8 0.2 copy.14
  277.9 0.2 fusion.25
  278.1 123.5 %psum.37 = f32[32,15]{1,0:T(8,128)S(1)} all-reduce(f32[32,15]{1,0:T(8,128)S(1)} %bitcast.54), channel_id=1, replica_groups=mesh['pop'=16,'tp'=32] {'tp'}, use_global_device_ids=true, to_apply=%region_2.4 | all-reduce | flops 480 | bytes 3840 | tf_op jit(solution)/shard_map/psum | solution.py:37
  401.7 3.3 fusion.42
  405.0 0.2 divide_convert_fusion
  405.2 0.2 fusion.15
  405.4 0.2 copy.24
  405.6 67.7 %psum.38 = f32[32]{0:T(128)S(1)} all-reduce(f32[32]{0:T(128)S(1)} %fusion.30), channel_id=1, replica_groups=mesh['pop'=16,'tp'=32] {'tp'}, use_global_device_ids=true, to_apply=%region_4.6 | all-reduce | flops 32 | bytes 256 | tf_op jit(solution)/shard_map/psum | solution.py:48
  473.3 0.5 add_add_fusion.3
  473.8 3.2 fusion
  477.0 133.7 %all-reduce.2.cloned.1.call-done = f32[4096,128]{1,0:T(8,128)} async-done(((f32[4096,128]{1,0:T(8,128)}), f32[4096,128]{1,0:T(8,128)}) %all-reduce.2.cloned.1.call-update) | async-done | bytes 2097168 | tf_op jit(solution)/shard_map/psum | solution.py:54
  610.7 2.7 multiply_convert_fusion
  (38 shorter events, 0.4 us)
Async XLA Ops:
  7.2 131.8 %copy-start = (bf16[4096,128]{1,0:T(8,128)(2,1)S(1)}, bf16[4096,128]{1,0:T(8,128)(2,1)}, u32[]{:S(2)}) copy-start(bf16[4096,128]{1,0:T(8,128)(2,1)} %param.13) | copy-start | bytes 3145732
  7.2 3.6 copy-start.3
  7.2 4.4 copy-start.4
  7.2 4.5 copy-start.1
  7.2 131.8 %all-gather.5.cloned.1.call-start = ((), (), s32[]{:S(2)}) async-start(), calls=%async_computation | async-start | bytes 4055040 | tf_op jit(solution)/shard_map/all_gather | solution.py:30
  11.6 257.2 %all-gather.7.cloned.1.call-start = ((), (), s32[]{:S(2)}) async-start(), calls=%async_computation.1 | async-start | bytes 4055040 | tf_op jit(solution)/shard_map/all_gather | solution.py:30
  143.0 130.6 %all-gather.11.cloned.1.call-start = ((), (), s32[]{:S(2)}) async-start(), calls=%async_computation.3 | async-start | bytes 2162688 | tf_op jit(solution)/shard_map/all_gather | solution.py:50
  143.7 257.9 %all-gather.9.cloned.1.call-start = ((), (), s32[]{:S(2)}) async-start(), calls=%async_computation.2 | async-start | bytes 4055040 | tf_op jit(solution)/shard_map/all_gather | solution.py:30
  268.8 7.6 %copy-start.2 = (f32[128]{0:T(128)S(1)}, f32[128]{0:T(128)}, u32[]{:S(2)}) copy-start(f32[128]{0:T(128)} %param.16) | copy-start | bytes 1540
  272.8 337.9 %all-reduce.2.cloned.1.call-start = ((), (), s32[]{:S(2)}) async-start(), calls=%async_computation.4 | async-start | bytes 4194304 | tf_op jit(solution)/shard_map/psum | solution.py:54
  277.9 195.3 %copy-start.5 = (s32[32]{0:T(128)S(1)}, s32[32]{0:T(128)}, u32[]{:S(2)}) copy-start(s32[32]{0:T(128)} %param.19) | copy-start | bytes 388
Sparse Core Ops, SparseCore 0:
  11.7 69.6 all-gather.4
  143.1 67.6 all-gather.6
  213.9 59.6 all-gather.10
  277.1 63.5 all-gather.8
  477.1 133.5 all-reduce.1
where the time goes:
time: 628 us; the launch traced here: 620 us
  blocking collectives  441 us (70%)
  waiting for transfers between devices  135 us (21%)
  matrix products  17.5 us (3%)
  between operations  14.1 us (2%)
  other arithmetic  6.33 us (1%)
    psum x3, blocking collectives, shards(): projection = lax.psum(partial_proj, 'tp')  373 us
    psum x1, waiting for transfers between devices, shards(): grad_total = lax.psum(partial_grad, 'pop')  134 us
    psum x1, blocking collectives, shards(): lax.psum(jnp.sum(readout_sum, axis=1), 'tp') / (episodes * step_count)  67.7 us
  transfers between devices with their start and end apart: 5, of which 2 were waited for; matrix products, arithmetic and copies ran while one was open for 2% of the time, Pallas kernels for 0%

commit v1 on v0

v1 whole, which is shorter than its diff:
```python
import functools

import jax
import jax.numpy as jnp
from jax import lax
from jax.experimental import pallas as pl
from jax.experimental.pallas import tpu as pltpu
from jax.sharding import PartitionSpec as P

MESH = pl.DeviceIdType.MESH
F32 = jnp.float32
BF16 = jnp.bfloat16
sigma_scale = 0.01

STEPS = 4
EPIS = 15
EP = 16
SIDE = 4
CHIPS = 16
TP = 32
COLS = 128
PAIR = 256
HALF = 16
ROWS = EPIS * HALF
NEUR = 4096
KTAB = 256

NT = (((1,), (1,)), ((), ()))
TN = (((0,), (0,)), ((), ()))


def dot(left, right):
    return jnp.dot(left, right, preferred_element_type=F32)


def dot_nt(left, right):
    return lax.dot_general(left, right, NT, preferred_element_type=F32)


def squash(membrane):
    return (0.5 + 0.5 * jnp.tanh(2.0 * membrane - 2.0)).astype(BF16)


def kernel(
    pops,
    in_hbm,
    w_in_hbm,
    w_rec_hbm,
    leak_ref,
    bias_ref,
    readout_ref,
    table_hbm,
    idx_ref,
    rank_ref,
    returns_ref,
    grad_hbm,
    spk_v,
    w_in_v,
    w_pair,
    x_v,
    table_v,
    tt_all,
    m1_src,
    m1,
    m2,
    pair_v,
    meta,
    m3,
    m4,
    proj_v,
    lhs_v,
    acc_v,
    accp_v,
    mem_v,
    spikes_v,
    post_all,
    grad_v,
    local_sem,
    out_sem,
    m1_send,
    m1_recv,
    m2_send,
    m2_recv,
    m3_send,
    m3_recv,
    m4_send,
    m4_recv,
    meta_send,
    meta_recv,
    pair_send,
    pair_recv,
    tt_send,
    tt_recv,
    sp_send,
    sp_recv,
):
    pop = lax.axis_index("pop")
    me = lax.axis_index("tp")
    core = lax.rem(me, 2)
    chip = lax.div(me, 2)
    mate = me + 1 - 2 * core
    groups = max(1, pops // 4)

    loads = [
        pltpu.make_async_copy(src, dst, local_sem.at[i])
        for i, (src, dst) in enumerate(
            (
                (in_hbm, spk_v),
                (w_in_hbm, w_in_v),
                (table_hbm, table_v),
                (w_rec_hbm, w_pair.at[core]),
            )
        )
    ]
    for load in loads:
        load.start()

    barrier = pltpu.get_barrier_semaphore()

    def greet_plane(k, _):
        pl.semaphore_signal(
            barrier, inc=1, device_id=(pop, lax.rem(me + k, TP)), device_id_type=MESH
        )
        return 0

    lax.fori_loop(1, TP, greet_plane, 0)

    def greet_pop(k, _):
        pl.semaphore_signal(
            barrier, inc=1, device_id=(lax.rem(pop + k, pops), me), device_id_type=MESH
        )
        return 0

    if pops > 1:
        lax.fori_loop(1, pops, greet_pop, 0)

    lane = lax.broadcasted_iota(jnp.int32, (32, 128), 1)
    member = lax.broadcasted_iota(jnp.int32, (32, 128), 0)
    here = lane == member + lax.rem(pop, 4) * 32
    pre_idx = idx_ref[:, 0:1]
    post_idx = idx_ref[:, 1:2]
    pre_row = jnp.sum(jnp.where(here, pre_idx.astype(F32), 0.0), axis=0, keepdims=True)
    post_row = jnp.sum(jnp.where(here, post_idx.astype(F32), 0.0), axis=0, keepdims=True)
    meta[pop, 0:1, :] = pre_row
    meta[pop, 1:2, :] = post_row
    meta[pop, 2:8, :] = jnp.zeros((6, 128), F32)

    loads[2].wait()
    spot = lax.broadcasted_iota(jnp.int32, (32, KTAB), 1)
    pick = jnp.concatenate(
        [
            jnp.where(spot == pre_idx, 1.0, 0.0).astype(BF16),
            jnp.where(spot == post_idx, 1.0, 0.0).astype(BF16),
        ],
        axis=0,
    )
    picked = dot(pick, table_v[...]).astype(BF16)
    for half in range(2):
        m1_src[half, 16:32, :] = picked[16 * half : 16 * half + 16]
        m1_src[half, 32:48, :] = picked[32 + 16 * half : 48 + 16 * half]
    tt_all[core, chip] = table_v[...].astype(F32).T.astype(BF16)

    loads[0].wait()
    for t in range(STEPS):
        rows = spk_v[t].astype(F32)
        x_v[EP * t : EP * (t + 1), :] = jnp.concatenate(
            [rows, jnp.zeros((EP - EPIS, NEUR), F32)], axis=0
        ).astype(BF16)
    loads[1].wait()
    drive = dot(x_v[...], w_in_v[...]) + bias_ref[...]
    drive0 = drive[0:16]
    drive1 = drive[16:32]
    pair_v[core, 0:32, :] = drive[32:64]
    pair_v[core, 32:40, :] = jnp.broadcast_to(leak_ref[...], (8, 128))
    pair_v[core, 40:48, :] = jnp.broadcast_to(readout_ref[...], (8, 128))
    spikes0 = squash(drive0)
    m1_src[0, 0:16, :] = spikes0
    m1_src[1, 0:16, :] = spikes0
    m1[me] = m1_src[core]

    pl.semaphore_wait(barrier, TP - 1 + pops - 1)

    def send_m1(k, _):
        peer = lax.rem(me + k, TP)
        pltpu.make_async_remote_copy(
            src_ref=m1_src.at[lax.rem(peer, 2)],
            dst_ref=m1.at[me],
            send_sem=m1_send,
            recv_sem=m1_recv,
            device_id=(pop, peer),
            device_id_type=MESH,
        ).start()
        return 0

    lax.fori_loop(1, TP, send_m1, 0)

    to_mate = [
        pltpu.make_async_remote_copy(
            src_ref=src,
            dst_ref=dst,
            send_sem=pair_send.at[i],
            recv_sem=pair_recv.at[i],
            device_id=(pop, mate),
            device_id_type=MESH,
        )
        for i, (src, dst) in enumerate(
            (
                (pair_v.at[core], pair_v.at[core]),
                (w_rec_hbm, w_pair.at[core]),
                (tt_all.at[core], tt_all.at[core]),
            )
        )
    ]
    to_mate[0].start()
    to_mate[1].start()

    first = lax.rem(chip, SIDE) * (1 - core) + lax.div(chip, SIDE) * core
    second = lax.div(chip, SIDE) * (1 - core) + lax.rem(chip, SIDE) * core

    def chip_at(u, v):
        return (u * (1 - core) + v * core) + SIDE * (v * (1 - core) + u * core)

    def step(w, by):
        return lax.rem(w + by, SIDE)

    across = [first, step(first, 3), step(first, 1), step(first, 2)]
    v_minus, v_plus, v_far = step(second, 3), step(second, 1), step(second, 2)

    def gather_ops(ref, low, send_sem, recv_sem):
        total = ref.shape[1]

        def part(slot, half):
            if half == 0:
                return ref.at[slot, pl.ds(0, low)]
            if half == 1:
                return ref.at[slot, pl.ds(low, total - low)]
            return ref.at[slot]

        def send(slot, to, sem, half=None):
            pltpu.make_async_remote_copy(
                src_ref=part(slot, half),
                dst_ref=part(slot, half),
                send_sem=send_sem,
                recv_sem=recv_sem.at[sem],
                device_id=(pop, 2 * to + core),
                device_id_type=MESH,
            ).start()

        def wait(slot, sem, half=None):
            piece = part(slot, half)
            pltpu.make_async_copy(piece, piece, recv_sem.at[sem]).wait()

        def along(i):
            slot = chip_at(across[i], second)
            send(slot, chip_at(first, v_plus), 4 + 4 * i)
            send(slot, chip_at(first, v_minus), 5 + 4 * i)

        def begin():
            slot = chip_at(first, second)
            send(slot, chip_at(across[2], second), 0)
            send(slot, chip_at(across[1], second), 1)
            along(0)

        def near(i):
            slot = chip_at(across[i], second)
            wait(slot, i - 1)
            send(slot, chip_at(across[3 - i], second), 1 + i, half=i - 1)
            along(i)
            return slot

        def far():
            slot = chip_at(across[3], second)
            wait(slot, 2, half=0)
            wait(slot, 3, half=1)
            along(3)
            return slot

        def side_minus(i):
            slot = chip_at(across[i], v_minus)
            wait(slot, 4 + 4 * i)
            send(slot, chip_at(first, v_plus), 6 + 4 * i, half=0)
            return slot

        def side_plus(i):
            slot = chip_at(across[i], v_plus)
            wait(slot, 5 + 4 * i)
            send(slot, chip_at(first, v_minus), 7 + 4 * i, half=1)
            return slot

        def last(i):
            slot = chip_at(across[i], v_far)
            wait(slot, 6 + 4 * i, half=0)
            wait(slot, 7 + 4 * i, half=1)
            return slot

        def finish():
            sent = ref.at[pl.ds(0, CHIPS - 1)]
            pltpu.make_async_copy(sent, sent, send_sem).wait()

        return begin, near, far, side_minus, side_plus, last, finish

    tt_ref = tt_all.at[core]
    tt_begin, tt_near, tt_far, tt_minus, tt_plus, tt_last, tt_finish = gather_ops(
        tt_ref, 64, tt_send, tt_recv
    )
    tt_begin()

    def send_meta(k, _):
        pltpu.make_async_remote_copy(
            src_ref=meta.at[pop],
            dst_ref=meta.at[pop],
            send_sem=meta_send,
            recv_sem=meta_recv,
            device_id=(lax.rem(pop + k, pops), me),
            device_id_type=MESH,
        ).start()
        return 0

    if pops > 1:
        lax.fori_loop(1, pops, send_meta, 0)

    loads[3].wait()
    others = m1.at[pl.ds(0, TP - 1)]
    pltpu.make_async_copy(others, others, m1_recv).wait()

    def both(ref, c, low, high):
        return jnp.concatenate([ref[2 * c, low:high, :], ref[2 * c + 1, low:high, :]], axis=1)

    recurrent1 = jnp.zeros((16, COLS), F32)
    for c in range(CHIPS):
        recurrent1 = recurrent1 + dot(
            both(m1, c, 0, 16), w_pair[core, pl.ds(PAIR * c, PAIR), :]
        )
    m2[me] = leak_ref[...] * (drive0 - spikes0.astype(F32)) + (drive1 + recurrent1)

    def send_m2(k, _):
        pltpu.make_async_remote_copy(
            src_ref=m2.at[me],
            dst_ref=m2.at[me],
            send_sem=m2_send,
            recv_sem=m2_recv,
            device_id=(pop, lax.rem(me + k, TP)),
            device_id_type=MESH,
        ).start()
        return 0

    lax.fori_loop(1, TP, send_m2, 0)

    project1 = jnp.zeros((HALF, EP), F32)
    for c in range(CHIPS):
        project1 = project1 + dot_nt(both(m1, c, 16, 32), both(m1, c, 0, 16))
    for e in range(EPIS):
        proj_v[e] = jnp.broadcast_to(sigma_scale * project1[:, e : e + 1], (HALF, 128))

    tt_near(1)
    tt_near(2)
    tt_minus(0)
    tt_plus(0)

    to_mate[0].wait_recv()
    to_mate[1].wait_recv()
    others2 = m2.at[pl.ds(0, TP - 1)]
    pltpu.make_async_copy(others2, others2, m2_recv).wait()

    acc_v[...] = jnp.zeros_like(acc_v)
    accp_v[...] = jnp.zeros_like(accp_v)

    def weights(c):
        rows = pl.ds(pl.multiple_of(PAIR * c, PAIR), PAIR)
        return jnp.concatenate([w_pair[0, rows, :], w_pair[1, rows, :]], axis=1)

    def spread(e):
        return jnp.concatenate([proj_v[e], proj_v[e]], axis=1)

    def step2(i, _):
        for k in range(2):
            c = 2 * i + k
            base = 2.0 * both(m2, c, 0, 16) - 2.0
            post = 2.0 * both(m1, c, 32, 48).astype(F32)
            for e in range(EPIS):
                lhs_v[k, HALF * e : HALF * (e + 1), :] = (
                    0.5 + 0.5 * jnp.tanh(base[e : e + 1] + spread(e) * post)
                ).astype(BF16)
        for k in range(2):
            c = 2 * i + k
            acc_v[...] += dot(lhs_v[k], weights(c))
            accp_v[...] += dot_nt(lhs_v[k], both(m1, c, 16, 32))
        return 0

    lax.fori_loop(0, CHIPS // 2, step2, 0)

    leak = jnp.concatenate([pair_v[0, 32:33, :], pair_v[1, 32:33, :]], axis=1)
    readout = jnp.concatenate([pair_v[0, 40:41, :], pair_v[1, 40:41, :]], axis=1)
    drive2 = jnp.concatenate([pair_v[0, 0:16, :], pair_v[1, 0:16, :]], axis=1)
    drive3 = jnp.concatenate([pair_v[0, 16:32, :], pair_v[1, 16:32, :]], axis=1)
    post_here = both(m1, chip, 32, 48).astype(F32)
    base_here = both(m2, chip, 0, 16)
    eye = lax.broadcasted_iota(jnp.int32, (HALF, HALF), 0) == lax.broadcasted_iota(
        jnp.int32, (HALF, HALF), 1
    )

    def projection(e):
        square = accp_v[HALF * e : HALF * (e + 1), :]
        own = jnp.sum(jnp.where(eye, square, 0.0), axis=1, keepdims=True)
        return sigma_scale * own * post_here

    first_spikes = both(m1, chip, 0, 16).astype(F32)
    real = lax.broadcasted_iota(jnp.int32, (EP, PAIR), 0) < EPIS
    spike_sum = jnp.broadcast_to(
        jnp.sum(jnp.where(real, first_spikes, 0.0), axis=0, keepdims=True), (HALF, PAIR)
    )
    for e in range(EPIS):
        rows = slice(HALF * e, HALF * (e + 1))
        membrane1 = base_here[e : e + 1] + spread(e) * post_here
        spikes1 = squash(membrane1).astype(F32)
        membrane2 = leak * (membrane1 - spikes1) + (
            drive2[e : e + 1] + acc_v[rows, :] + projection(e)
        )
        spikes2 = squash(membrane2)
        spikes_v[chip, rows, :] = spikes2
        wide = spikes2.astype(F32)
        spike_sum = spike_sum + (spikes1 + wide)
        mem_v[rows, :] = leak * (membrane2 - wide) + drive3[e : e + 1]

    sp_begin, sp_near, sp_far, sp_minus, sp_plus, sp_last, sp_finish = gather_ops(
        spikes_v, 128, sp_send, sp_recv
    )
    sp_begin()

    acc_v[...] = jnp.zeros_like(acc_v)
    accp_v[...] = jnp.zeros_like(accp_v)

    def take(c):
        block = spikes_v[c]
        acc_v[...] += dot(block, weights(c))
        accp_v[...] += dot_nt(block, both(m1, c, 16, 32))

    tt_far()
    take(chip)
    take(sp_near(1))
    take(sp_near(2))
    take(sp_minus(0))
    take(sp_plus(0))
    take(sp_far())
    tt_minus(1)
    tt_plus(1)
    tt_minus(2)
    tt_plus(2)
    take(sp_minus(1))
    take(sp_plus(1))
    take(sp_minus(2))
    take(sp_plus(2))
    take(sp_last(0))
    tt_minus(3)
    tt_plus(3)
    take(sp_minus(3))
    take(sp_plus(3))

    if pops > 1:
        others3 = meta.at[pl.ds(0, pops - 1)]
        pltpu.make_async_copy(others3, others3, meta_recv).wait()
    slot_of = lax.broadcasted_iota(jnp.int32, (KTAB, 128), 0).astype(F32)
    per_group = min(4, pops)

    def group_row(ref, g, row):
        total = ref[per_group * g, row : row + 1, :]
        for k in range(1, per_group):
            total = total + ref[per_group * g + k, row : row + 1, :]
        return total

    for g in range(groups):
        chosen = jnp.where(slot_of == group_row(meta, g, 1), 1.0, 0.0)
        post_all[128 * g : 128 * (g + 1), :] = dot(
            chosen.T.astype(BF16), table_v[...]
        ).astype(BF16)

    take(sp_last(1))
    take(sp_last(2))
    take(sp_last(3))

    for e in range(EPIS):
        rows = slice(HALF * e, HALF * (e + 1))
        membrane3 = mem_v[rows, :] + (acc_v[rows, :] + projection(e))
        spike_sum = spike_sum + squash(membrane3).astype(F32)

    reward = jnp.sum(spike_sum * readout, axis=1, keepdims=True)
    lane16 = lax.broadcasted_iota(jnp.int32, (HALF, 128), 1)
    member16 = lax.broadcasted_iota(jnp.int32, (HALF, 128), 0)
    mine = lane16 == member16 + (lax.rem(pop, 4) * 32 + core * HALF)
    m3[me] = jnp.sum(jnp.where(mine, reward, 0.0), axis=0, keepdims=True)

    def send_m3(k, _):
        pltpu.make_async_remote_copy(
            src_ref=m3.at[me],
            dst_ref=m3.at[me],
            send_sem=m3_send,
            recv_sem=m3_recv,
            device_id=(pop, lax.rem(me + k, TP)),
            device_id_type=MESH,
        ).start()
        return 0

    lax.fori_loop(1, TP, send_m3, 0)

    for i in range(4):
        tt_last(i)
    to_mate[2].start()

    others4 = m3.at[pl.ds(0, TP - 1)]
    pltpu.make_async_copy(others4, others4, m3_recv).wait()
    returns_row = jnp.sum(m3[...], axis=0) / (EPIS * STEPS)
    returns_ref[...] = (
        returns_row[:, 0:32] + returns_row[:, 32:64] + returns_row[:, 64:96] + returns_row[:, 96:128]
    )
    ranks = rank_ref[...].astype(F32) / (32 * pops - 1) - 0.5
    ranks = jnp.concatenate([ranks, ranks, ranks, ranks], axis=1)
    lane1 = lax.broadcasted_iota(jnp.int32, (1, 128), 1)
    m4[pop] = jnp.where(lax.div(lane1, 32) == lax.rem(pop, 4), ranks + returns_row, 0.0)

    def send_m4(k, _):
        pltpu.make_async_remote_copy(
            src_ref=m4.at[pop],
            dst_ref=m4.at[pop],
            send_sem=m4_send,
            recv_sem=m4_recv,
            device_id=(lax.rem(pop + k, pops), me),
            device_id_type=MESH,
        ).start()
        return 0

    if pops > 1:
        lax.fori_loop(1, pops, send_m4, 0)
        others5 = m4.at[pl.ds(0, pops - 1)]
        pltpu.make_async_copy(others5, others5, m4_recv).wait()

    high, low = [], []
    for g in range(groups):
        scaled = jnp.where(slot_of == group_row(meta, g, 0), group_row(m4, g, 0), 0.0)
        top = scaled.astype(BF16)
        high.append(top)
        low.append((scaled - top.astype(F32)).astype(BF16))
    mixed = dot(jnp.concatenate(high, axis=1), post_all[...]) + dot(
        jnp.concatenate(low, axis=1), post_all[...]
    )
    mixed = mixed * jnp.sqrt(jnp.float32(12.0 / (32 * pops)))
    top = mixed.astype(BF16)
    split = jnp.concatenate([top, (mixed - top.astype(F32)).astype(BF16)], axis=1)

    to_mate[2].wait_recv()

    def grad_rows(c, _):
        for k in range(2):
            both_parts = dot(tt_all[k, c], split)
            start = pl.multiple_of(PAIR * c + COLS * k, COLS)
            grad_v[pl.ds(start, COLS), :] = (
                both_parts[:, 0:COLS] + both_parts[:, COLS:PAIR]
            ).astype(BF16)
        return 0

    stores = []
    for q in range(4):
        lax.fori_loop(4 * q, 4 * q + 4, grad_rows, 0)
        store = pltpu.make_async_copy(
            grad_v.at[pl.ds(1024 * q, 1024)], grad_hbm.at[pl.ds(1024 * q, 1024)], out_sem.at[q]
        )
        store.start()
        stores.append(store)

    tt_finish()
    sp_finish()
    pltpu.make_async_copy(others, others, m1_send).wait()
    pltpu.make_async_copy(others2, others2, m2_send).wait()
    pltpu.make_async_copy(others4, others4, m3_send).wait()
    if pops > 1:
        pltpu.make_async_copy(others3, others3, meta_send).wait()
        pltpu.make_async_copy(others5, others5, m4_send).wait()
    for copy in to_mate:
        copy.wait_send()
    for store in stores:
        store.wait()


def shards(
    in_spikes, w_in, w_rec, leak_rate, neuron_bias, readout, pert_table, pert_idx, member_ranks
):
    pops = lax.axis_size("pop")
    vmem = pl.BlockSpec(memory_space=pltpu.VMEM)
    hbm = pl.BlockSpec(memory_space=pl.ANY)
    dma = pltpu.SemaphoreType.DMA
    returns, grad_rec = pl.pallas_call(
        functools.partial(kernel, pops),
        out_shape=(
            jax.ShapeDtypeStruct((1, 32), F32),
            jax.ShapeDtypeStruct((NEUR, COLS), BF16),
        ),
        in_specs=[hbm, hbm, hbm, vmem, vmem, vmem, hbm, vmem, vmem],
        out_specs=(vmem, hbm),
        scratch_shapes=[
            pltpu.VMEM((STEPS, EPIS, NEUR), jnp.int32),
            pltpu.VMEM((NEUR, COLS), BF16),
            pltpu.VMEM((2, NEUR, COLS), BF16),
            pltpu.VMEM((STEPS * EP, NEUR), BF16),
            pltpu.VMEM((KTAB, COLS), BF16),
            pltpu.VMEM((2, CHIPS, COLS, KTAB), BF16),
            pltpu.VMEM((2, 48, COLS), BF16),
            pltpu.VMEM((TP, 48, COLS), BF16),
            pltpu.VMEM((TP, EP, COLS), F32),
            pltpu.VMEM((2, 48, COLS), F32),
            pltpu.VMEM((pops, 8, 128), F32),
            pltpu.VMEM((TP, 1, 128), F32),
            pltpu.VMEM((pops, 1, 128), F32),
            pltpu.VMEM((EPIS, HALF, 128), F32),
            pltpu.VMEM((2, ROWS, PAIR), BF16),
            pltpu.VMEM((ROWS, PAIR), F32),
            pltpu.VMEM((ROWS, HALF), F32),
            pltpu.VMEM((ROWS, PAIR), F32),
            pltpu.VMEM((CHIPS, ROWS, PAIR), BF16),
            pltpu.VMEM((128 * max(1, pops // 4), COLS), BF16),
            pltpu.VMEM((NEUR, COLS), BF16),
            dma((4,)),
            dma((4,)),
            dma,
            dma,
            dma,
            dma,
            dma,
            dma,
            dma,
            dma,
            dma,
            dma,
            dma((3,)),
            dma((3,)),
            dma,
            dma((20,)),
            dma,
            dma((20,)),
        ],
        compiler_params=pltpu.CompilerParams(
            collective_id=0, has_side_effects=True, vmem_limit_bytes=48 * 1024 * 1024
        ),
        name="rollout",
    )(
        in_spikes,
        w_in,
        w_rec,
        leak_rate.reshape(1, COLS),
        neuron_bias.reshape(1, COLS),
        readout.reshape(1, COLS),
        pert_table,
        pert_idx,
        member_ranks.reshape(1, 32),
    )
    return returns.reshape(32), grad_rec


def solution(mesh):
    placed = (
        P(),
        P(None, "tp"),
        P(None, "tp"),
        P("tp"),
        P("tp"),
        P("tp"),
        P(None, "tp"),
        P("pop", None),
        P("pop"),
    )
    return jax.shard_map(
        shards, mesh=mesh, in_specs=placed, out_specs=(P("pop"), P(None, "tp")), check_vma=False
    )
```

time: 628 us -> 73 us (0.12); the launches traced: 620 us -> 72.8 us
  blocking collectives: 441 us -> 0 us
  waiting for transfers between devices: 135 us -> 0 us
  Pallas kernels: 0 us -> 66.6 us
  matrix products: 17.5 us -> 0 us
  between operations: 14.1 us -> 0.72 us
  other arithmetic: 6.33 us -> 0 us
    psum x4 -> x0, blocking collectives: 441 us -> none  [the longest x3 373 us: shards(): projection = lax.psum(partial_proj, 'tp')]
    psum x1 -> x0, waiting for transfers between devices: 134 us -> none  [shards(): grad_total = lax.psum(partial_grad, 'pop')]
    pallas_call x0 -> x1, Pallas kernels: none -> 66.6 us  [shards(): pl.pallas_call(functools.partial(kernel, pops), out_shape=(jax.ShapeDtype...]
    dot_general x12 -> x0, matrix products: 17.5 us -> none  [the longest x3 11.3 us: shards(): jnp.dot(lax.all_gather(flat_spikes, 'tp', axis=1, tiled=True), w_rec, pre...]
  transfers between devices with their start and end apart: 5 -> 0, of which waited for: 2 -> 0; matrix products, arithmetic and copies ran while one was open for 2% -> 0% of each run, Pallas kernels for 0% -> 0%
where the time goes in v1:
time: 73 us; the launch traced here: 72.8 us
  Pallas kernels  66.6 us (91%)
  local copies, waits for them, and re-layouts  5.41 us (7%)
    pallas_call x1, Pallas kernels, shards(): pl.pallas_call(functools.partial(kernel, pops), out_shape=(jax.ShapeDtype...  66.6 us
    unnamed x18, local copies, waits for them, and re-layouts  5.41 us

profile of v1, /device:TPU:1, one launch (start us, length us, event | category | flops | bytes accessed | tf_op | source)
XLA Modules:
  0.0 72.8 jit_solution(1843887330611248582)
XLA Ops:
  0.6 0.0 copy-start
  0.6 0.8 %copy.12.idx_ref = s32[32,2]{1,0:T(8,128)S(1)} copy(s32[32,2]{0,1:T(2,128)} %param.16) | data formatting | bytes 512 | tf_op args[7]
  1.5 0.0 copy-start.2
  1.5 0.0 copy-start.3
  1.5 0.0 copy-start.4
  1.5 0.0 copy-start.5
  1.5 0.0 copy-start.6
  1.5 1.8 %copy.11.in_hbm = s32[4,15,4096]{2,1,0:T(8,128)S(1)} copy(s32[4,15,4096]{2,0,1:T(4,128)} %param.9) | data formatting | bytes 1966080 | tf_op args[0]
  3.4 0.0 copy-done
  3.4 0.0 copy-done.2
  3.4 0.0 copy-done.3
  3.4 0.0 copy-done.4
  3.4 0.0 copy-done.5
  3.4 0.0 copy-done.6
  3.4 0.0 copy-start.1
  3.4 1.2 %copy-done.1 = bf16[4096,128]{1,0:T(8,128)(2,1)S(1)} copy-done((bf16[4096,128]{1,0:T(8,128)(2,1)S(1)}, bf16[4096,128]{1,0:T(8,128)(2,1)}, u32[]{:S(2)}) %copy-start.1) | copy-done | bytes 1048600
  4.6 66.6 %rollout.1 = (f32[1,32]{1,0:T(1,128)S(1)}, bf16[4096,128]{1,0:T(8,128)(2,1)S(1)}) custom-call(s32[4,15,4096]{2,1,0:T(8,128)S(1)} %copy.11.in_hbm, bf16[4096,128]{1,0:T(8,128)(2,1)S(1)} %copy-done, bf16[4096,128]{1,0:T(8,128)(2,1)S(1)} %copy-done.1, f32[1,128]{1,0:T(1,128)S(1)} %bitcast.5, f32[1,128]{1,0:T(1,128)S(1)} %bitcast.6, f32[1,128]{1,0:T(1,128)S(1)} %bitcast.7, ...), custom_call_target="tpu_custom_call" | custom-call | tf_op jit(solution)/shard_map/rollout/pallas_call | solution.py:590
  71.3 0.5 copy.15
  71.8 1.0 %copy.16 = bf16[4096,128]{1,0:T(8,128)(2,1)} copy(bf16[4096,128]{1,0:T(8,128)(2,1)S(1)} %get-tuple-element.9) | data formatting | bytes 2097152
Async XLA Ops:
  0.6 2.7 %copy-start = (bf16[4096,128]{1,0:T(8,128)(2,1)S(1)}, bf16[4096,128]{1,0:T(8,128)(2,1)}, u32[]{:S(2)}) copy-start(bf16[4096,128]{1,0:T(8,128)(2,1)} %w_in_hbm.1) | copy-start | bytes 3145732
  1.5 1.9 %copy-start.2 = (bf16[256,128]{1,0:T(8,128)(2,1)S(1)}, bf16[256,128]{1,0:T(8,128)(2,1)}, u32[]{:S(2)}) copy-start(bf16[256,128]{1,0:T(8,128)(2,1)} %table_hbm.1) | copy-start | bytes 196612
  1.5 1.9 %copy-start.3 = (f32[128]{0:T(128)S(1)}, f32[128]{0:T(128)}, u32[]{:S(2)}) copy-start(f32[128]{0:T(128)} %param.12) | copy-start | bytes 1540
  1.5 1.9 %copy-start.4 = (f32[128]{0:T(128)S(1)}, f32[128]{0:T(128)}, u32[]{:S(2)}) copy-start(f32[128]{0:T(128)} %param.13) | copy-start | bytes 1540
  1.5 1.9 %copy-start.5 = (f32[128]{0:T(128)S(1)}, f32[128]{0:T(128)}, u32[]{:S(2)}) copy-start(f32[128]{0:T(128)} %param.14) | copy-start | bytes 1540
  1.5 1.9 %copy-start.6 = (s32[32]{0:T(128)S(1)}, s32[32]{0:T(128)}, u32[]{:S(2)}) copy-start(s32[32]{0:T(128)} %param.17) | copy-start | bytes 388
  3.4 1.2 %copy-start.1 = (bf16[4096,128]{1,0:T(8,128)(2,1)S(1)}, bf16[4096,128]{1,0:T(8,128)(2,1)}, u32[]{:S(2)}) copy-start(bf16[4096,128]{1,0:T(8,128)(2,1)} %w_rec_hbm.1) | copy-start | bytes 3145732

commit v2 on v1

v2 whole, which is shorter than its diff:
```python
import functools

import jax
import jax.numpy as jnp
from jax import lax
from jax.experimental import pallas as pl
from jax.experimental.pallas import tpu as pltpu
from jax.sharding import PartitionSpec as P

MESH = pl.DeviceIdType.MESH
F32 = jnp.float32
BF16 = jnp.bfloat16
sigma_scale = 0.01

STEPS = 4
EPIS = 15
EP = 16
SIDE = 4
CHIPS = 16
TP = 32
COLS = 128
PAIR = 256
HALF = 16
ROWS = EPIS * HALF
PIECES = 3
PIECE = ROWS // PIECES
NEUR = 4096
KTAB = 256

NT = (((1,), (1,)), ((), ()))
TN = (((0,), (0,)), ((), ()))


def dot(left, right):
    return jnp.dot(left, right, preferred_element_type=F32)


def dot_nt(left, right):
    return lax.dot_general(left, right, NT, preferred_element_type=F32)


def squash(membrane):
    return (0.5 + 0.5 * jnp.tanh(2.0 * membrane - 2.0)).astype(BF16)


def kernel(
    pops,
    in_hbm,
    w_in_hbm,
    w_rec_hbm,
    leak_ref,
    bias_ref,
    readout_ref,
    table_hbm,
    idx_ref,
    rank_ref,
    returns_ref,
    grad_ref,
    spk_v,
    w_in_v,
    w_pair,
    x_v,
    drive_v,
    table_v,
    tt_all,
    rows_src,
    rows_v,
    m1,
    m2,
    pair_v,
    meta,
    m3,
    m4,
    proj_v,
    lhs_v,
    acc_v,
    accp_v,
    mem_v,
    spikes_v,
    post_all,
    local_sem,
    m1_send,
    m1_recv,
    rows_send,
    rows_recv,
    m2_send,
    m2_recv,
    m3_send,
    m3_recv,
    m4_send,
    m4_recv,
    meta_send,
    meta_recv,
    pair_send,
    pair_recv,
    tt_send,
    tt_recv,
    sp_send,
    sp_recv,
):
    pop = lax.axis_index("pop")
    me = lax.axis_index("tp")
    core = lax.rem(me, 2)
    chip = lax.div(me, 2)
    mate = me + 1 - 2 * core
    groups = max(1, pops // 4)
    quarter = NEUR // 4
    parts = [pl.ds(quarter * q, quarter) for q in range(4)]
    loads = [pltpu.make_async_copy(table_hbm, table_v, local_sem.at[0])]
    for q, part in enumerate(parts):
        loads += [
            pltpu.make_async_copy(
                in_hbm.at[:, :, part], spk_v.at[:, :, part], local_sem.at[2 * q + 1]
            ),
            pltpu.make_async_copy(w_in_hbm.at[part], w_in_v.at[part], local_sem.at[2 * q + 2]),
        ]
    loads.append(pltpu.make_async_copy(w_rec_hbm, w_pair.at[core], local_sem.at[9]))
    for load in loads:
        load.start()

    arrivals, departures, background = {"w_rec": loads[9].wait}, [], []

    def bytes_of(ref, sem):
        return pltpu.make_async_copy(ref, ref, sem).wait

    def arrived(name):
        arrivals.pop(name)()

    def advance(count):
        for _ in range(count):
            background.pop(0)()

    def finish():
        advance(len(background))
        for name in list(arrivals):
            arrived(name)
        for departed in departures:
            departed()

    def exchanged(name, ref, peers, send_sem, recv_sem):
        part = ref.at[pl.ds(0, peers)]
        arrivals[name] = bytes_of(part, recv_sem)
        departures.append(bytes_of(part, send_sem))

    x, y = lax.rem(chip, SIDE), lax.div(chip, SIDE)

    def hops(shift, size):
        return min(shift, size - shift)

    shifts = sorted(
        ((dx, dy, dc) for dx in range(SIDE) for dy in range(SIDE) for dc in range(2)),
        key=lambda s: -(hops(s[0], SIDE) + hops(s[1], SIDE)),
    )
    plane = [
        (pop, 2 * (SIDE * lax.rem(y + dy, SIDE) + lax.rem(x + dx, SIDE)) + (1 - core if dc else core))
        for dx, dy, dc in shifts
        if dx + dy + dc > 0
    ]
    same_core = [dc == 0 for dx, dy, dc in shifts if dx + dy + dc > 0]
    column = [
        (lax.rem(pop + k, pops), me) for k in sorted(range(1, pops), key=lambda k: -hops(k, pops))
    ]

    barrier = pltpu.get_barrier_semaphore()
    for peer in column + plane:
        pl.semaphore_signal(barrier, inc=1, device_id=peer, device_id_type=MESH)

    def push(source, target, peers, send_sem, recv_sem, by_core=False):
        for n, peer in enumerate(peers):
            src = source
            if by_core:
                src = source.at[core if same_core[n] else 1 - core]
            pltpu.make_async_remote_copy(
                src_ref=src,
                dst_ref=target,
                send_sem=send_sem,
                recv_sem=recv_sem,
                device_id=peer,
                device_id_type=MESH,
            ).start()

    lane1 = lax.broadcasted_iota(jnp.int32, (1, 128), 1)
    here = lax.div(lane1, 32) == lax.rem(pop, 4)

    def placed(row):
        return jnp.where(here, jnp.concatenate([row, row, row, row], axis=1), 0.0)

    indices = idx_ref[...].astype(F32)
    meta[pop, 0:1, :] = placed(indices[0:1])
    meta[pop, 1:2, :] = placed(indices[1:2])
    meta[pop, 2:8, :] = jnp.zeros((6, 128), F32)

    loads[0].wait()
    spot = lax.broadcasted_iota(jnp.int32, (32, KTAB), 1).astype(F32)
    diagonal = lax.broadcasted_iota(jnp.int32, (32, 32), 0) == lax.broadcasted_iota(
        jnp.int32, (32, 32), 1
    )

    def picks(row):
        column = jnp.sum(jnp.where(diagonal, row, 0.0), axis=1, keepdims=True)
        return jnp.where(spot == column, 1.0, 0.0).astype(BF16)

    pick = jnp.concatenate([picks(indices[0:1]), picks(indices[1:2])], axis=0)
    picked = dot(pick, table_v[...]).astype(BF16)
    for half in range(2):
        rows_src[half, 0:16, :] = picked[16 * half : 16 * half + 16]
        rows_src[half, 16:32, :] = picked[32 + 16 * half : 48 + 16 * half]
    rows_v[me] = rows_src[core]
    tt_all[core, chip] = table_v[...].astype(F32).T.astype(BF16)

    drive = jnp.broadcast_to(bias_ref[...], (STEPS * EP, COLS))
    x_v[STEPS * EPIS :, :] = jnp.zeros((STEPS, NEUR), F32)
    for q, part in enumerate(parts):
        loads[2 * q + 1].wait()
        for e in range(EPIS):
            x_v[STEPS * e : STEPS * (e + 1), part] = spk_v[e, :, part].astype(F32)
        loads[2 * q + 2].wait()
        drive = drive + dot(x_v[:, part].astype(BF16), w_in_v[part, :])
    drive_v[...] = drive

    def drive_at(t):
        return drive_v[pl.ds(t, EP, stride=STEPS), :]

    drive0 = drive_at(0)
    drive1 = drive_at(1)
    pair_v[core, 0:16, :] = drive_at(2)
    pair_v[core, 16:32, :] = drive_at(3)
    pair_v[core, 32:40, :] = jnp.broadcast_to(leak_ref[...], (8, 128))
    pair_v[core, 40:48, :] = jnp.broadcast_to(readout_ref[...], (8, 128))
    spikes0 = squash(drive0)
    m1[me] = spikes0

    pl.semaphore_wait(barrier, TP - 1 + pops - 1)


    push(m1.at[me], m1.at[me], plane, m1_send, m1_recv)
    exchanged("m1", m1, TP - 1, m1_send, m1_recv)
    push(rows_src, rows_v.at[me], plane, rows_send, rows_recv, by_core=True)
    exchanged("rows", rows_v, TP - 1, rows_send, rows_recv)

    to_mate = [
        pltpu.make_async_remote_copy(
            src_ref=src,
            dst_ref=dst,
            send_sem=pair_send.at[i],
            recv_sem=pair_recv.at[i],
            device_id=(pop, mate),
            device_id_type=MESH,
        )
        for i, (src, dst) in enumerate(
            (
                (pair_v.at[core], pair_v.at[core]),
                (w_rec_hbm, w_pair.at[core]),
                (tt_all.at[core], tt_all.at[core]),
            )
        )
    ]
    def start_mate(i):
        to_mate[i].start()
        arrivals["mate%d" % i] = to_mate[i].wait_recv
        departures.append(to_mate[i].wait_send)

    start_mate(0)
    start_mate(1)

    first = lax.rem(chip, SIDE) * (1 - core) + lax.div(chip, SIDE) * core
    second = lax.div(chip, SIDE) * (1 - core) + lax.rem(chip, SIDE) * core

    def chip_at(u, v):
        return (u * (1 - core) + v * core) + SIDE * (v * (1 - core) + u * core)

    def step(w, by):
        return lax.rem(w + by, SIDE)

    across = [first, step(first, 3), step(first, 1), step(first, 2)]
    v_minus, v_plus, v_far = step(second, 3), step(second, 1), step(second, 2)

    def gather_ops(ref, start, low, total, send_sem, recv_sem):
        def part(slot, half):
            if half == 0:
                return ref.at[slot, pl.ds(start, low)]
            if half == 1:
                return ref.at[slot, pl.ds(start + low, total - low)]
            return ref.at[slot, pl.ds(start, total)]

        def send(slot, to, sem, half=None):
            pltpu.make_async_remote_copy(
                src_ref=part(slot, half),
                dst_ref=part(slot, half),
                send_sem=send_sem,
                recv_sem=recv_sem.at[sem],
                device_id=(pop, 2 * to + core),
                device_id_type=MESH,
            ).start()

        def wait(slot, sem, half=None):
            piece = part(slot, half)
            pltpu.make_async_copy(piece, piece, recv_sem.at[sem]).wait()

        def along(i):
            slot = chip_at(across[i], second)
            send(slot, chip_at(first, v_plus), 4 + 4 * i)
            send(slot, chip_at(first, v_minus), 5 + 4 * i)

        def near(i):
            slot = chip_at(across[i], second)
            wait(slot, i - 1)
            send(slot, chip_at(across[3 - i], second), 1 + i, half=i - 1)
            along(i)
            return slot

        def far():
            slot = chip_at(across[3], second)
            wait(slot, 2, half=0)
            wait(slot, 3, half=1)
            along(3)
            return slot

        def side_minus(i):
            slot = chip_at(across[i], v_minus)
            wait(slot, 4 + 4 * i)
            send(slot, chip_at(first, v_plus), 6 + 4 * i, half=0)
            return slot

        def side_plus(i):
            slot = chip_at(across[i], v_plus)
            wait(slot, 5 + 4 * i)
            send(slot, chip_at(first, v_minus), 7 + 4 * i, half=1)
            return slot

        def last(i):
            slot = chip_at(across[i], v_far)
            wait(slot, 6 + 4 * i, half=0)
            wait(slot, 7 + 4 * i, half=1)
            return slot

        def begin():
            slot = chip_at(first, second)
            send(slot, chip_at(across[2], second), 0)
            send(slot, chip_at(across[1], second), 1)
            along(0)

        return begin, near, far, side_minus, side_plus, last

    tt_ref = tt_all.at[core]
    tt_begin, tt_near, tt_far, tt_minus, tt_plus, tt_last = gather_ops(
        tt_ref, 0, 64, COLS, tt_send, tt_recv
    )
    tt_begin()
    departures.append(bytes_of(tt_ref.at[pl.ds(0, CHIPS - 1)], tt_send))
    background += [
        lambda: tt_near(1),
        lambda: tt_near(2),
        lambda: tt_minus(0),
        lambda: tt_plus(0),
        lambda: tt_far(),
        lambda: tt_minus(1),
        lambda: tt_plus(1),
        lambda: tt_minus(2),
        lambda: tt_plus(2),
        lambda: tt_minus(3),
        lambda: tt_plus(3),
        lambda: tt_last(0),
        lambda: tt_last(1),
        lambda: tt_last(2),
        lambda: tt_last(3),
        lambda: start_mate(2),
    ]

    if pops > 1:
        push(meta.at[pop], meta.at[pop], column, meta_send, meta_recv)
        exchanged("meta", meta, pops - 1, meta_send, meta_recv)

    arrived("w_rec")
    arrived("m1")

    def both(ref, c, low, high):
        return jnp.concatenate([ref[2 * c, low:high, :], ref[2 * c + 1, low:high, :]], axis=1)

    recurrent1 = jnp.zeros((16, COLS), F32)
    for c in range(CHIPS):
        recurrent1 = recurrent1 + dot(
            both(m1, c, 0, 16), w_pair[core, pl.ds(PAIR * c, PAIR), :]
        )
    m2[me] = leak_ref[...] * (drive0 - spikes0.astype(F32)) + (drive1 + recurrent1)

    push(m2.at[me], m2.at[me], plane, m2_send, m2_recv)
    exchanged("m2", m2, TP - 1, m2_send, m2_recv)

    advance(4)
    arrived("rows")
    project1 = jnp.zeros((HALF, EP), F32)
    for c in range(CHIPS):
        project1 = project1 + dot_nt(both(rows_v, c, 0, 16), both(m1, c, 0, 16))
    for e in range(EPIS):
        proj_v[e] = jnp.broadcast_to(sigma_scale * project1[:, e : e + 1], (HALF, 128))

    advance(1)

    arrived("mate0")
    arrived("mate1")
    arrived("m2")

    advance(4)
    acc_v[...] = jnp.zeros_like(acc_v)
    accp_v[...] = jnp.zeros_like(accp_v)

    def weights(c):
        rows = pl.ds(pl.multiple_of(PAIR * c, PAIR), PAIR)
        return jnp.concatenate([w_pair[0, rows, :], w_pair[1, rows, :]], axis=1)

    def spread(e):
        return jnp.concatenate([proj_v[e], proj_v[e]], axis=1)

    def step2(i, _):
        for k in range(2):
            c = 2 * i + k
            base = 2.0 * both(m2, c, 0, 16) - 2.0
            post = 2.0 * both(rows_v, c, 16, 32).astype(F32)
            for e in range(EPIS):
                lhs_v[k, HALF * e : HALF * (e + 1), :] = (
                    0.5 + 0.5 * jnp.tanh(base[e : e + 1] + spread(e) * post)
                ).astype(BF16)
        for k in range(2):
            c = 2 * i + k
            acc_v[...] += dot(lhs_v[k], weights(c))
            accp_v[...] += dot_nt(lhs_v[k], both(rows_v, c, 0, 16))
        return 0

    lax.fori_loop(0, CHIPS // 2, step2, 0)

    slot_of = lax.broadcasted_iota(jnp.int32, (KTAB, 128), 0).astype(F32)
    per_group = min(4, pops)

    def group_row(ref, g, row):
        total = ref[per_group * g, row : row + 1, :]
        for k in range(1, per_group):
            total = total + ref[per_group * g + k, row : row + 1, :]
        return total

    def choose_posts():
        if pops > 1:
            arrived("meta")
        for g in range(groups):
            chosen = jnp.where(slot_of == group_row(meta, g, 1), 1.0, 0.0)
            post_all[128 * g : 128 * (g + 1), :] = dot(
                chosen.T.astype(BF16), table_v[...]
            ).astype(BF16)

    leak = jnp.concatenate([pair_v[0, 32:33, :], pair_v[1, 32:33, :]], axis=1)
    readout = jnp.concatenate([pair_v[0, 40:41, :], pair_v[1, 40:41, :]], axis=1)
    drive2 = jnp.concatenate([pair_v[0, 0:16, :], pair_v[1, 0:16, :]], axis=1)
    drive3 = jnp.concatenate([pair_v[0, 16:32, :], pair_v[1, 16:32, :]], axis=1)
    post_here = both(rows_v, chip, 16, 32).astype(F32)
    base_here = both(m2, chip, 0, 16)
    eye = lax.broadcasted_iota(jnp.int32, (HALF, HALF), 0) == lax.broadcasted_iota(
        jnp.int32, (HALF, HALF), 1
    )

    def projection(e):
        square = accp_v[HALF * e : HALF * (e + 1), :]
        own = jnp.sum(jnp.where(eye, square, 0.0), axis=1, keepdims=True)
        return sigma_scale * own * post_here

    first_spikes = both(m1, chip, 0, 16).astype(F32)
    real = lax.broadcasted_iota(jnp.int32, (EP, PAIR), 0) < EPIS
    spike_sum = jnp.broadcast_to(
        jnp.sum(jnp.where(real, first_spikes, 0.0), axis=0, keepdims=True), (HALF, PAIR)
    )
    pieces = [
        gather_ops(spikes_v, PIECE * q, 48, PIECE, sp_send, sp_recv.at[q]) for q in range(PIECES)
    ]
    departures.append(bytes_of(spikes_v.at[pl.ds(0, CHIPS - 1)], sp_send))
    for e in range(EPIS):
        rows = slice(HALF * e, HALF * (e + 1))
        membrane1 = base_here[e : e + 1] + spread(e) * post_here
        spikes1 = squash(membrane1).astype(F32)
        membrane2 = leak * (membrane1 - spikes1) + (
            drive2[e : e + 1] + acc_v[rows, :] + projection(e)
        )
        spikes2 = squash(membrane2)
        spikes_v[chip, rows, :] = spikes2
        wide = spikes2.astype(F32)
        spike_sum = spike_sum + (spikes1 + wide)
        mem_v[rows, :] = leak * (membrane2 - wide) + drive3[e : e + 1]
        if (e + 1) * HALF % PIECE == 0:
            pieces[e * HALF // PIECE][0]()

    acc_v[...] = jnp.zeros_like(acc_v)
    accp_v[...] = jnp.zeros_like(accp_v)

    def take(c):
        block = spikes_v[c]
        acc_v[...] += dot(block, weights(c))
        accp_v[...] += dot_nt(block, both(rows_v, c, 0, 16))

    advance(2)
    take(chip)
    order = [(1, 1), (1, 2), (3, 0), (4, 0), (2, None), (3, 1), (4, 1), (3, 2), (4, 2), (5, 0), (3, 3)]
    order += [(4, 3), (5, 1), (5, 2), (5, 3)]
    events = sorted((i + 4 * q, q, op) for q in range(PIECES) for i, op in enumerate(order))
    for when, (_, q, (kind, which)) in enumerate(events):
        slot = pieces[q][kind]() if which is None else pieces[q][kind](which)
        if q == PIECES - 1:
            take(slot)
        if when == len(events) // 2:
            choose_posts()

    for e in range(EPIS):
        rows = slice(HALF * e, HALF * (e + 1))
        membrane3 = mem_v[rows, :] + (acc_v[rows, :] + projection(e))
        spike_sum = spike_sum + squash(membrane3).astype(F32)

    reward = jnp.sum(spike_sum * readout, axis=1, keepdims=True)
    lane16 = lax.broadcasted_iota(jnp.int32, (HALF, 128), 1)
    member16 = lax.broadcasted_iota(jnp.int32, (HALF, 128), 0)
    mine = lane16 == member16 + (lax.rem(pop, 4) * 32 + core * HALF)
    m3[me] = jnp.sum(jnp.where(mine, reward, 0.0), axis=0, keepdims=True)

    push(m3.at[me], m3.at[me], plane, m3_send, m3_recv)
    exchanged("m3", m3, TP - 1, m3_send, m3_recv)

    advance(5)

    arrived("m3")
    returns_row = jnp.sum(m3[...], axis=0) / (EPIS * STEPS)
    returns_ref[...] = (
        returns_row[:, 0:32] + returns_row[:, 32:64] + returns_row[:, 64:96] + returns_row[:, 96:128]
    )
    ranks = rank_ref[...].astype(F32) / (32 * pops - 1) - 0.5
    m4[pop] = placed(ranks) + returns_row

    if pops > 1:
        push(m4.at[pop], m4.at[pop], column, m4_send, m4_recv)
        exchanged("m4", m4, pops - 1, m4_send, m4_recv)
        arrived("m4")

    high, low = [], []
    for g in range(groups):
        scaled = jnp.where(slot_of == group_row(meta, g, 0), group_row(m4, g, 0), 0.0)
        top = scaled.astype(BF16)
        high.append(top)
        low.append((scaled - top.astype(F32)).astype(BF16))
    mixed = dot(jnp.concatenate(high, axis=1), post_all[...]) + dot(
        jnp.concatenate(low, axis=1), post_all[...]
    )
    mixed = mixed * jnp.sqrt(jnp.float32(12.0 / (32 * pops)))
    top = mixed.astype(BF16)
    split = jnp.concatenate([top, (mixed - top.astype(F32)).astype(BF16)], axis=1)

    arrived("mate2")

    for k in range(2):
        for q in range(4):
            block = tt_all[k, 4 * q : 4 * q + 4].reshape(4 * COLS, KTAB)
            both_parts = dot(block, split)
            rows = (both_parts[:, 0:COLS] + both_parts[:, COLS:PAIR]).astype(BF16)
            for n in range(4):
                start = PAIR * (4 * q + n) + COLS * k
                grad_ref[start : start + COLS, :] = rows[COLS * n : COLS * (n + 1)]

    finish()


def shards(
    in_spikes, w_in, w_rec, leak_rate, neuron_bias, readout, pert_table, pert_idx, member_ranks
):
    pops = lax.axis_size("pop")
    vmem = pl.BlockSpec(memory_space=pltpu.VMEM)
    hbm = pl.BlockSpec(memory_space=pltpu.HBM)
    dma = pltpu.SemaphoreType.DMA
    returns, grad_rec = pl.pallas_call(
        functools.partial(kernel, pops),
        out_shape=(
            jax.ShapeDtypeStruct((1, 32), F32),
            jax.ShapeDtypeStruct((NEUR, COLS), BF16),
        ),
        in_specs=[hbm, hbm, hbm, vmem, vmem, vmem, hbm, vmem, vmem],
        out_specs=(vmem, vmem),
        scratch_shapes=[
            pltpu.VMEM((EPIS, STEPS, NEUR), jnp.int32),
            pltpu.VMEM((NEUR, COLS), BF16),
            pltpu.VMEM((2, NEUR, COLS), BF16),
            pltpu.VMEM((STEPS * EP, NEUR), F32),
            pltpu.VMEM((STEPS * EP, COLS), F32),
            pltpu.VMEM((KTAB, COLS), BF16),
            pltpu.VMEM((2, CHIPS, COLS, KTAB), BF16),
            pltpu.VMEM((2, 32, COLS), BF16),
            pltpu.VMEM((TP, 32, COLS), BF16),
            pltpu.VMEM((TP, EP, COLS), BF16),
            pltpu.VMEM((TP, EP, COLS), F32),
            pltpu.VMEM((2, 48, COLS), F32),
            pltpu.VMEM((pops, 8, 128), F32),
            pltpu.VMEM((TP, 1, 128), F32),
            pltpu.VMEM((pops, 1, 128), F32),
            pltpu.VMEM((EPIS, HALF, 128), F32),
            pltpu.VMEM((2, ROWS, PAIR), BF16),
            pltpu.VMEM((ROWS, PAIR), F32),
            pltpu.VMEM((ROWS, HALF), F32),
            pltpu.VMEM((ROWS, PAIR), F32),
            pltpu.VMEM((CHIPS, ROWS, PAIR), BF16),
            pltpu.VMEM((128 * max(1, pops // 4), COLS), BF16),
            dma((10,)),
            dma,
            dma,
            dma,
            dma,
            dma,
            dma,
            dma,
            dma,
            dma,
            dma,
            dma,
            dma,
            dma((3,)),
            dma((3,)),
            dma,
            dma((20,)),
            dma,
            dma((PIECES, 20)),
        ],
        compiler_params=pltpu.CompilerParams(
            collective_id=0, has_side_effects=True, vmem_limit_bytes=60 * 1024 * 1024
        ),
        name="rollout",
    )(
        in_spikes.transpose(1, 0, 2),
        w_in,
        w_rec,
        leak_rate.reshape(1, COLS),
        neuron_bias.reshape(1, COLS),
        readout.reshape(1, COLS),
        pert_table,
        pert_idx.T,
        member_ranks.reshape(1, 32),
    )
    return returns.reshape(32), grad_rec


def solution(mesh):
    placed = (
        P(),
        P(None, "tp"),
        P(None, "tp"),
        P("tp"),
        P("tp"),
        P("tp"),
        P(None, "tp"),
        P("pop", None),
        P("pop"),
    )
    return jax.shard_map(
        shards, mesh=mesh, in_specs=placed, out_specs=(P("pop"), P(None, "tp")), check_vma=False
    )
```

time: 73 us -> 72.6 us (level)
  local copies, waits for them, and re-layouts: 5.41 us -> 3.39 us
  Pallas kernels: 66.6 us -> 68.3 us
    unnamed x18 -> x4, local copies, waits for them, and re-layouts: 5.41 us -> 3.39 us
    pallas_call x1, Pallas kernels: 66.6 us -> 68.3 us  [shards(): pl.pallas_call(functools.partial(kernel, pops), out_shape=(jax.ShapeDtype...]
where the time goes in v2:
time: 72.6 us; the launch traced here: 72.4 us
  Pallas kernels  68.3 us (94%)
  local copies, waits for them, and re-layouts  3.39 us (5%)
    pallas_call x1, Pallas kernels, shards(): pl.pallas_call(functools.partial(kernel, pops), out_shape=(jax.ShapeDtype...  68.3 us
    unnamed x4, local copies, waits for them, and re-layouts  3.39 us

profile of v2, /device:TPU:1, one launch (start us, length us, event | category | flops | bytes accessed | tf_op | source)
XLA Modules:
  0.0 72.4 jit_solution(4850098992285367890)
XLA Ops:
  0.6 68.3 %rollout.1 = (f32[1,32]{1,0:T(1,128)}, bf16[4096,128]{1,0:T(8,128)(2,1)}) custom-call(s32[15,4,4096]{2,1,0:T(4,128)} %bitcast.7, bf16[4096,128]{1,0:T(8,128)(2,1)} %w_in_hbm.1, bf16[4096,128]{1,0:T(8,128)(2,1)} %w_rec_hbm.1, f32[1,128]{1,0:T(1,128)} %bitcast.9, f32[1,128]{1,0:T(1,128)} %bitcast.10, f32[1,128]{1,0:T(1,128)} %bitcast.11, ...), custom_call_target="tpu_custom_call" | custom-call | tf_op jit(solution)/shard_map/rollout/pallas_call | solution.py:572
  69.0 0.0 copy-start
  69.0 0.6 copy-done
  69.6 0.5 copy.13
  70.1 2.3 %copy.14 = bf16[4096,128]{1,0:T(8,128)(2,1)} copy(bf16[4096,128]{1,0:T(8,128)(2,1)} %get-tuple-element.9) | data formatting | bytes 2097152
Async XLA Ops:
  69.0 0.6 copy-start

commit v3 on v2

--- a/solution.py
+++ b/solution.py
@@ -24,6 +24,7 @@
 ROWS = EPIS * HALF
 PIECES = 3
 PIECE = ROWS // PIECES
+LOW = 48
 NEUR = 4096
 KTAB = 256
 
@@ -55,14 +56,14 @@
     idx_ref,
     rank_ref,
     returns_ref,
-    grad_ref,
+    tt_all,
+    split_ref,
     spk_v,
     w_in_v,
     w_pair,
     x_v,
     drive_v,
     table_v,
-    tt_all,
     rows_src,
     rows_v,
     m1,
@@ -251,10 +252,10 @@
             (
                 (pair_v.at[core], pair_v.at[core]),
                 (w_rec_hbm, w_pair.at[core]),
-                (tt_all.at[core], tt_all.at[core]),
             )
         )
     ]
+
     def start_mate(i):
         to_mate[i].start()
         arrivals["mate%d" % i] = to_mate[i].wait_recv
@@ -302,18 +303,20 @@
             send(slot, chip_at(first, v_plus), 4 + 4 * i)
             send(slot, chip_at(first, v_minus), 5 + 4 * i)
 
-        def near(i):
+        def near(i, onward=True):
             slot = chip_at(across[i], second)
             wait(slot, i - 1)
             send(slot, chip_at(across[3 - i], second), 1 + i, half=i - 1)
-            along(i)
+            if onward:
+                along(i)
             return slot
 
-        def far():
+        def far(onward=True):
             slot = chip_at(across[3], second)
             wait(slot, 2, half=0)
             wait(slot, 3, half=1)
-            along(3)
+            if onward:
+                along(3)
             return slot
 
         def side_minus(i):
@@ -334,37 +337,56 @@
             wait(slot, 7 + 4 * i, half=1)
             return slot
 
-        def begin():
+        def begin(onward=True):
             slot = chip_at(first, second)
             send(slot, chip_at(across[2], second), 0)
             send(slot, chip_at(across[1], second), 1)
-            along(0)
-
-        return begin, near, far, side_minus, side_plus, last
+            if onward:
+                along(0)
+
+        return begin, near, far, side_minus, side_plus, last, along
 
     tt_ref = tt_all.at[core]
-    tt_begin, tt_near, tt_far, tt_minus, tt_plus, tt_last = gather_ops(
+    tt_begin, tt_near, tt_far, tt_minus, tt_plus, tt_last, tt_along = gather_ops(
         tt_ref, 0, 64, COLS, tt_send, tt_recv
     )
-    tt_begin()
+    tt_begin(onward=False)
     departures.append(bytes_of(tt_ref.at[pl.ds(0, CHIPS - 1)], tt_send))
+    departures.append(bytes_of(tt_ref, pair_send.at[2]))
+    arrivals["mate2"] = bytes_of(tt_ref, pair_recv.at[2])
+
+    def share(slot):
+        pltpu.make_async_remote_copy(
+            src_ref=tt_all.at[core, slot],
+            dst_ref=tt_all.at[core, slot],
+            send_sem=pair_send.at[2],
+            recv_sem=pair_recv.at[2],
+            device_id=(pop, mate),
+            device_id_type=MESH,
+        ).start()
+
+    def tt_second():
+        for i in range(SIDE):
+            tt_along(i)
+        for i in range(SIDE):
+            share(chip_at(across[i], second))
+
+    def tt_sides():
+        for i in range(SIDE):
+            share(tt_minus(i))
+            share(tt_plus(i))
+
+    def tt_rest():
+        for i in range(SIDE):
+            share(tt_last(i))
+
     background += [
-        lambda: tt_near(1),
-        lambda: tt_near(2),
-        lambda: tt_minus(0),
-        lambda: tt_plus(0),
-        lambda: tt_far(),
-        lambda: tt_minus(1),
-        lambda: tt_plus(1),
-        lambda: tt_minus(2),
-        lambda: tt_plus(2),
-        lambda: tt_minus(3),
-        lambda: tt_plus(3),
-        lambda: tt_last(0),
-        lambda: tt_last(1),
-        lambda: tt_last(2),
-        lambda: tt_last(3),
-        lambda: start_mate(2),
+        lambda: tt_near(1, onward=False),
+        lambda: tt_near(2, onward=False),
+        lambda: tt_far(onward=False),
+        tt_second,
+        tt_sides,
+        tt_rest,
     ]
 
     if pops > 1:
@@ -387,7 +409,7 @@
     push(m2.at[me], m2.at[me], plane, m2_send, m2_recv)
     exchanged("m2", m2, TP - 1, m2_send, m2_recv)
 
-    advance(4)
+    advance(2)
     arrived("rows")
     project1 = jnp.zeros((HALF, EP), F32)
     for c in range(CHIPS):
@@ -401,7 +423,6 @@
     arrived("mate1")
     arrived("m2")
 
-    advance(4)
     acc_v[...] = jnp.zeros_like(acc_v)
     accp_v[...] = jnp.zeros_like(accp_v)
 
@@ -468,7 +489,7 @@
         jnp.sum(jnp.where(real, first_spikes, 0.0), axis=0, keepdims=True), (HALF, PAIR)
     )
     pieces = [
-        gather_ops(spikes_v, PIECE * q, 48, PIECE, sp_send, sp_recv.at[q]) for q in range(PIECES)
+        gather_ops(spikes_v, PIECE * q, LOW, PIECE, sp_send, sp_recv.at[q]) for q in range(PIECES)
     ]
     departures.append(bytes_of(spikes_v.at[pl.ds(0, CHIPS - 1)], sp_send))
     for e in range(EPIS):
@@ -494,12 +515,13 @@
         acc_v[...] += dot(block, weights(c))
         accp_v[...] += dot_nt(block, both(rows_v, c, 0, 16))
 
-    advance(2)
     take(chip)
     order = [(1, 1), (1, 2), (3, 0), (4, 0), (2, None), (3, 1), (4, 1), (3, 2), (4, 2), (5, 0), (3, 3)]
     order += [(4, 3), (5, 1), (5, 2), (5, 3)]
-    events = sorted((i + 4 * q, q, op) for q in range(PIECES) for i, op in enumerate(order))
-    for when, (_, q, (kind, which)) in enumerate(events):
+    stage = [0] * 4 + [1] * 5 + [2] * 3 + [3] * 3
+    events = sorted((stage[i], q, i) for q in range(PIECES) for i in range(len(order)))
+    for when, (_, q, i) in enumerate(events):
+        kind, which = order[i]
         slot = pieces[q][kind]() if which is None else pieces[q][kind](which)
         if q == PIECES - 1:
             take(slot)
@@ -520,7 +542,7 @@
     push(m3.at[me], m3.at[me], plane, m3_send, m3_recv)
     exchanged("m3", m3, TP - 1, m3_send, m3_recv)
 
-    advance(5)
+    advance(1)
 
     arrived("m3")
     returns_row = jnp.sum(m3[...], axis=0) / (EPIS * STEPS)
@@ -533,6 +555,8 @@
     if pops > 1:
         push(m4.at[pop], m4.at[pop], column, m4_send, m4_recv)
         exchanged("m4", m4, pops - 1, m4_send, m4_recv)
+    advance(2)
+    if pops > 1:
         arrived("m4")
 
     high, low = [], []
@@ -546,20 +570,27 @@
     )
     mixed = mixed * jnp.sqrt(jnp.float32(12.0 / (32 * pops)))
     top = mixed.astype(BF16)
-    split = jnp.concatenate([top, (mixed - top.astype(F32)).astype(BF16)], axis=1)
-
+    split_ref[...] = jnp.concatenate([top, (mixed - top.astype(F32)).astype(BF16)], axis=1)
     arrived("mate2")
-
-    for k in range(2):
-        for q in range(4):
-            block = tt_all[k, 4 * q : 4 * q + 4].reshape(4 * COLS, KTAB)
-            both_parts = dot(block, split)
+    finish()
+
+
+def gradient(returns_in, tt_ref, split_ref, returns_ref, grad_hbm, grad_v, sems):
+    returns_ref[...] = returns_in[...]
+    stores = []
+    for q in range(CHIPS // 4):
+        for k in range(2):
+            block = tt_ref[k, 4 * q : 4 * q + 4].reshape(4 * COLS, KTAB)
+            both_parts = dot(block, split_ref[...])
             rows = (both_parts[:, 0:COLS] + both_parts[:, COLS:PAIR]).astype(BF16)
             for n in range(4):
                 start = PAIR * (4 * q + n) + COLS * k
-                grad_ref[start : start + COLS, :] = rows[COLS * n : COLS * (n + 1)]
-
-    finish()
+                grad_v[start : start + COLS, :] = rows[COLS * n : COLS * (n + 1)]
+        part = pl.ds(4 * PAIR * q, 4 * PAIR)
+        stores.append(pltpu.make_async_copy(grad_v.at[part], grad_hbm.at[part], sems.at[q]))
+        stores[-1].start()
+    for store in stores:
+        store.wait()
 
 
 def shards(
@@ -569,14 +600,15 @@
     vmem = pl.BlockSpec(memory_space=pltpu.VMEM)
     hbm = pl.BlockSpec(memory_space=pltpu.HBM)
     dma = pltpu.SemaphoreType.DMA
-    returns, grad_rec = pl.pallas_call(
+    returns, table_t, split = pl.pallas_call(
         functools.partial(kernel, pops),
         out_shape=(
             jax.ShapeDtypeStruct((1, 32), F32),
-            jax.ShapeDtypeStruct((NEUR, COLS), BF16),
+            jax.ShapeDtypeStruct((2, CHIPS, COLS, KTAB), BF16),
+            jax.ShapeDtypeStruct((KTAB, PAIR), BF16),
         ),
         in_specs=[hbm, hbm, hbm, vmem, vmem, vmem, hbm, vmem, vmem],
-        out_specs=(vmem, vmem),
+        out_specs=(vmem, vmem, vmem),
         scratch_shapes=[
             pltpu.VMEM((EPIS, STEPS, NEUR), jnp.int32),
             pltpu.VMEM((NEUR, COLS), BF16),
@@ -584,7 +616,6 @@
             pltpu.VMEM((STEPS * EP, NEUR), F32),
             pltpu.VMEM((STEPS * EP, COLS), F32),
             pltpu.VMEM((KTAB, COLS), BF16),
-            pltpu.VMEM((2, CHIPS, COLS, KTAB), BF16),
             pltpu.VMEM((2, 32, COLS), BF16),
             pltpu.VMEM((TP, 32, COLS), BF16),
             pltpu.VMEM((TP, EP, COLS), BF16),
@@ -621,7 +652,7 @@
             dma((PIECES, 20)),
         ],
         compiler_params=pltpu.CompilerParams(
-            collective_id=0, has_side_effects=True, vmem_limit_bytes=60 * 1024 * 1024
+            collective_id=0, has_side_effects=True, vmem_limit_bytes=53 * 1024 * 1024
         ),
         name="rollout",
     )(
@@ -635,6 +666,18 @@
         pert_idx.T,
         member_ranks.reshape(1, 32),
     )
+    returns, grad_rec = pl.pallas_call(
+        gradient,
+        out_shape=(
+            jax.ShapeDtypeStruct((1, 32), F32),
+            jax.ShapeDtypeStruct((NEUR, COLS), BF16),
+        ),
+        in_specs=[vmem, vmem, vmem],
+        out_specs=(vmem, hbm),
+        scratch_shapes=[pltpu.VMEM((NEUR, COLS), BF16), dma((CHIPS // 4,))],
+        compiler_params=pltpu.CompilerParams(vmem_limit_bytes=20 * 1024 * 1024),
+        name="gradient",
+    )(returns, table_t, split)
     return returns.reshape(32), grad_rec
 
 

time: 72.6 us -> 69.9 us (0.963)
  Pallas kernels: 68.3 us -> 63.3 us
  local copies, waits for them, and re-layouts: 3.39 us -> 5.71 us
    pallas_call x1, Pallas kernels: 68.3 us -> 61.3 us  [shards(): pl.pallas_call(functools.partial(kernel, pops), out_shape=(jax.ShapeDtype...]
    unnamed x4 -> x14, local copies, waits for them, and re-layouts: 3.39 us -> 5.71 us
    pallas_call x0 -> x1, Pallas kernels: none -> 1.96 us  [shards(): pl.pallas_call(gradient, out_shape=(jax.ShapeDtypeStruct((1, 32), F32), j...]
where the time goes in v3:
time: 69.9 us; the launch traced here: 69.7 us
  Pallas kernels  63.3 us (91%)
  local copies, waits for them, and re-layouts  5.71 us (8%)
    pallas_call x1, Pallas kernels, shards(): pl.pallas_call(functools.partial(kernel, pops), out_shape=(jax.ShapeDtype...  61.3 us
    unnamed x14, local copies, waits for them, and re-layouts  5.71 us
    pallas_call x1, Pallas kernels, shards(): pl.pallas_call(gradient, out_shape=(jax.ShapeDtypeStruct((1, 32), F32), j...  1.96 us

profile of v3, /device:TPU:1, one launch (start us, length us, event | category | flops | bytes accessed | tf_op | source)
XLA Modules:
  0.0 69.7 jit_solution(17173710207669470679)
XLA Ops:
  0.6 0.0 copy-start.1
  0.6 0.8 %copy-done.1 = bf16[256,128]{1,0:T(8,128)(2,1)S(1)} copy-done((bf16[256,128]{1,0:T(8,128)(2,1)S(1)}, bf16[256,128]{1,0:T(8,128)(2,1)}, u32[]{:S(2)}) %copy-start.1) | copy-done | bytes 65560
  1.5 0.0 copy-start.2
  1.5 0.7 copy-done.2
  2.2 0.0 copy-start.3
  2.2 0.7 copy-done.3
  2.8 0.0 copy-start.4
  2.8 0.7 copy-done.4
  3.5 0.0 copy-start.5
  3.5 0.7 copy-done.5
  4.1 0.0 copy-start.6
  4.1 0.7 copy-done.6
  4.8 61.3 %rollout.1 = (f32[1,32]{1,0:T(1,128)S(1)}, bf16[2,16,128,256]{3,2,1,0:T(8,128)(2,1)}, bf16[256,256]{1,0:T(8,128)(2,1)S(1)}) custom-call(s32[15,4,4096]{2,1,0:T(4,128)} %bitcast.12, bf16[4096,128]{1,0:T(8,128)(2,1)} %w_in_hbm.1, bf16[4096,128]{1,0:T(8,128)(2,1)} %w_rec_hbm.1, f32[1,128]{1,0:T(1,128)S(1)} %bitcast.8, f32[1,128]{1,0:T(1,128)S(1)} %bitcast.9, ...), custom_call_target="tpu_custom_call" | custom-call | tf_op jit(solution)/shard_map/rollout/pallas_call | solution.py:603
  66.1 0.0 copy-start
  66.1 1.6 %copy-done = bf16[2,16,128,256]{3,2,1,0:T(8,128)(2,1)S(1)} copy-done((bf16[2,16,128,256]{3,2,1,0:T(8,128)(2,1)S(1)}, bf16[2,16,128,256]{3,2,1,0:T(8,128)(2,1)}, u32[]{:S(2)}) %copy-start) | copy-done | bytes 2097176
  67.7 2.0 %gradient.1 = (f32[1,32]{1,0:T(1,128)}, bf16[4096,128]{1,0:T(8,128)(2,1)}) custom-call(f32[1,32]{1,0:T(1,128)S(1)} %get-tuple-element.7.returns_in, bf16[2,16,128,256]{3,2,1,0:T(8,128)(2,1)S(1)} %copy-done, bf16[256,256]{1,0:T(8,128)(2,1)S(1)} %get-tuple-element.9.split_ref), custom_call_target="tpu_custom_call" | custom-call | tf_op jit(solution)/shard_map/gradient/pallas_call | solution.py:669
Async XLA Ops:
  0.6 0.8 %copy-start.1 = (bf16[256,128]{1,0:T(8,128)(2,1)S(1)}, bf16[256,128]{1,0:T(8,128)(2,1)}, u32[]{:S(2)}) copy-start(bf16[256,128]{1,0:T(8,128)(2,1)} %table_hbm.1) | copy-start | bytes 196612
  1.5 0.7 copy-start.2
  2.2 0.7 copy-start.3
  2.8 0.7 copy-start.4
  3.5 0.7 copy-start.5
  4.1 0.7 copy-start.6
  66.1 1.6 %copy-start = (bf16[2,16,128,256]{3,2,1,0:T(8,128)(2,1)S(1)}, bf16[2,16,128,256]{3,2,1,0:T(8,128)(2,1)}, u32[]{:S(2)}) copy-start(bf16[2,16,128,256]{3,2,1,0:T(8,128)(2,1)} %get-tuple-element.8.tt_ref) | copy-start | bytes 6291460

commit v4 on v3

--- a/solution.py
+++ b/solution.py
@@ -49,15 +49,21 @@
     in_hbm,
     w_in_hbm,
     w_rec_hbm,
+    leak_hbm,
+    bias_hbm,
+    readout_hbm,
+    table_hbm,
+    idx_hbm,
+    rank_hbm,
+    returns_ref,
+    tt_hbm,
+    split_ref,
     leak_ref,
     bias_ref,
     readout_ref,
-    table_hbm,
     idx_ref,
     rank_ref,
-    returns_ref,
     tt_all,
-    split_ref,
     spk_v,
     w_in_v,
     w_pair,
@@ -116,7 +122,20 @@
             pltpu.make_async_copy(w_in_hbm.at[part], w_in_v.at[part], local_sem.at[2 * q + 2]),
         ]
     loads.append(pltpu.make_async_copy(w_rec_hbm, w_pair.at[core], local_sem.at[9]))
-    for load in loads:
+    small = [
+        pltpu.make_async_copy(src, dst, local_sem.at[10 + i])
+        for i, (src, dst) in enumerate(
+            (
+                (idx_hbm, idx_ref),
+                (leak_hbm, leak_ref),
+                (bias_hbm, bias_ref),
+                (readout_hbm, readout_ref),
+                (rank_hbm, rank_ref),
+            )
+        )
+    ]
+    small[0].start()
+    for load in loads + small[1:]:
         load.start()
 
     arrivals, departures, background = {"w_rec": loads[9].wait}, [], []
@@ -186,6 +205,7 @@
     def placed(row):
         return jnp.where(here, jnp.concatenate([row, row, row, row], axis=1), 0.0)
 
+    small[0].wait()
     indices = idx_ref[...].astype(F32)
     meta[pop, 0:1, :] = placed(indices[0:1])
     meta[pop, 1:2, :] = placed(indices[1:2])
@@ -209,6 +229,8 @@
     rows_v[me] = rows_src[core]
     tt_all[core, chip] = table_v[...].astype(F32).T.astype(BF16)
 
+    for load in small[1:]:
+        load.wait()
     drive = jnp.broadcast_to(bias_ref[...], (STEPS * EP, COLS))
     x_v[STEPS * EPIS :, :] = jnp.zeros((STEPS, NEUR), F32)
     for q, part in enumerate(parts):
@@ -556,6 +578,13 @@
         push(m4.at[pop], m4.at[pop], column, m4_send, m4_recv)
         exchanged("m4", m4, pops - 1, m4_send, m4_recv)
     advance(2)
+    saves = [
+        pltpu.make_async_copy(tt_all.at[part], tt_hbm.at[part], local_sem.at[15 + i])
+        for i, part in enumerate((core, 1 - core))
+    ]
+    saves[0].start()
+    arrived("mate2")
+    saves[1].start()
     if pops > 1:
         arrived("m4")
 
@@ -571,23 +600,34 @@
     mixed = mixed * jnp.sqrt(jnp.float32(12.0 / (32 * pops)))
     top = mixed.astype(BF16)
     split_ref[...] = jnp.concatenate([top, (mixed - top.astype(F32)).astype(BF16)], axis=1)
-    arrived("mate2")
+    for save in saves:
+        save.wait()
     finish()
 
 
-def gradient(returns_in, tt_ref, split_ref, returns_ref, grad_hbm, grad_v, sems):
+def gradient(returns_in, tt_hbm, split_ref, returns_ref, grad_hbm, tt_v, grad_v, in_sems, out_sems):
+    blocks = CHIPS // 4
+    loads = [
+        pltpu.make_async_copy(
+            tt_hbm.at[:, pl.ds(4 * q, 4)], tt_v.at[:, pl.ds(4 * q, 4)], in_sems.at[q]
+        )
+        for q in range(blocks)
+    ]
+    for load in loads:
+        load.start()
     returns_ref[...] = returns_in[...]
     stores = []
-    for q in range(CHIPS // 4):
+    for q in range(blocks):
+        loads[q].wait()
         for k in range(2):
-            block = tt_ref[k, 4 * q : 4 * q + 4].reshape(4 * COLS, KTAB)
+            block = tt_v[k, 4 * q : 4 * q + 4].reshape(4 * COLS, KTAB)
             both_parts = dot(block, split_ref[...])
             rows = (both_parts[:, 0:COLS] + both_parts[:, COLS:PAIR]).astype(BF16)
             for n in range(4):
                 start = PAIR * (4 * q + n) + COLS * k
                 grad_v[start : start + COLS, :] = rows[COLS * n : COLS * (n + 1)]
         part = pl.ds(4 * PAIR * q, 4 * PAIR)
-        stores.append(pltpu.make_async_copy(grad_v.at[part], grad_hbm.at[part], sems.at[q]))
+        stores.append(pltpu.make_async_copy(grad_v.at[part], grad_hbm.at[part], out_sems.at[q]))
         stores[-1].start()
     for store in stores:
         store.wait()
@@ -607,9 +647,15 @@
             jax.ShapeDtypeStruct((2, CHIPS, COLS, KTAB), BF16),
             jax.ShapeDtypeStruct((KTAB, PAIR), BF16),
         ),
-        in_specs=[hbm, hbm, hbm, vmem, vmem, vmem, hbm, vmem, vmem],
-        out_specs=(vmem, vmem, vmem),
+        in_specs=[hbm] * 9,
+        out_specs=(vmem, hbm, vmem),
         scratch_shapes=[
+            pltpu.VMEM((1, COLS), F32),
+            pltpu.VMEM((1, COLS), F32),
+            pltpu.VMEM((1, COLS), F32),
+            pltpu.VMEM((2, 32), jnp.int32),
+            pltpu.VMEM((1, 32), jnp.int32),
+            pltpu.VMEM((2, CHIPS, COLS, KTAB), BF16),
             pltpu.VMEM((EPIS, STEPS, NEUR), jnp.int32),
             pltpu.VMEM((NEUR, COLS), BF16),
             pltpu.VMEM((2, NEUR, COLS), BF16),
@@ -631,7 +677,7 @@
             pltpu.VMEM((ROWS, PAIR), F32),
             pltpu.VMEM((CHIPS, ROWS, PAIR), BF16),
             pltpu.VMEM((128 * max(1, pops // 4), COLS), BF16),
-            dma((10,)),
+            dma((17,)),
             dma,
             dma,
             dma,
@@ -652,7 +698,7 @@
             dma((PIECES, 20)),
         ],
         compiler_params=pltpu.CompilerParams(
-            collective_id=0, has_side_effects=True, vmem_limit_bytes=53 * 1024 * 1024
+            collective_id=0, has_side_effects=True, vmem_limit_bytes=60 * 1024 * 1024
         ),
         name="rollout",
     )(
@@ -672,10 +718,15 @@
             jax.ShapeDtypeStruct((1, 32), F32),
             jax.ShapeDtypeStruct((NEUR, COLS), BF16),
         ),
-        in_specs=[vmem, vmem, vmem],
+        in_specs=[vmem, hbm, vmem],
         out_specs=(vmem, hbm),
-        scratch_shapes=[pltpu.VMEM((NEUR, COLS), BF16), dma((CHIPS // 4,))],
-        compiler_params=pltpu.CompilerParams(vmem_limit_bytes=20 * 1024 * 1024),
+        scratch_shapes=[
+            pltpu.VMEM((2, CHIPS, COLS, KTAB), BF16),
+            pltpu.VMEM((NEUR, COLS), BF16),
+            dma((CHIPS // 4,)),
+            dma((CHIPS // 4,)),
+        ],
+        compiler_params=pltpu.CompilerParams(vmem_limit_bytes=60 * 1024 * 1024),
         name="gradient",
     )(returns, table_t, split)
     return returns.reshape(32), grad_rec

time: 69.9 us -> 66.9 us (0.957)
  local copies, waits for them, and re-layouts: 5.71 us -> 0 us
  Pallas kernels: 63.3 us -> 66 us
    unnamed x14 -> x0, local copies, waits for them, and re-layouts: 5.71 us -> none
    pallas_call x1, Pallas kernels: 1.96 us -> 4.44 us  [shards(): pl.pallas_call(gradient, out_shape=(jax.ShapeDtypeStruct((1, 32), F32), j...]
where the time goes in v4:
time: 66.9 us; the launch traced here: 66.7 us
  Pallas kernels  66 us (99%)
    pallas_call x1, Pallas kernels, shards(): pl.pallas_call(functools.partial(kernel, pops), out_shape=(jax.ShapeDtype...  61.6 us
    pallas_call x1, Pallas kernels, shards(): pl.pallas_call(gradient, out_shape=(jax.ShapeDtypeStruct((1, 32), F32), j...  4.44 us

profile of v4, /device:TPU:1, one launch (start us, length us, event | category | flops | bytes accessed | tf_op | source)
XLA Modules:
  0.0 66.7 jit_solution(13863221122737233071)
XLA Ops:
  0.6 61.6 %rollout.1 = (f32[1,32]{1,0:T(1,128)}, bf16[2,16,128,256]{3,2,1,0:T(8,128)(2,1)}, bf16[256,256]{1,0:T(8,128)(2,1)}) custom-call(s32[15,4,4096]{2,1,0:T(4,128)} %bitcast.7, bf16[4096,128]{1,0:T(8,128)(2,1)} %w_in_hbm.1, bf16[4096,128]{1,0:T(8,128)(2,1)} %w_rec_hbm.1, f32[1,128]{1,0:T(1,128)} %bitcast.9, f32[1,128]{1,0:T(1,128)} %bitcast.10, ...), custom_call_target="tpu_custom_call" | custom-call | tf_op jit(solution)/shard_map/rollout/pallas_call | solution.py:643
  62.2 4.4 %gradient.1 = (f32[1,32]{1,0:T(1,128)}, bf16[4096,128]{1,0:T(8,128)(2,1)}) custom-call(f32[1,32]{1,0:T(1,128)} %get-tuple-element.7.returns_in, bf16[2,16,128,256]{3,2,1,0:T(8,128)(2,1)} %get-tuple-element.8.tt_hbm, bf16[256,256]{1,0:T(8,128)(2,1)} %get-tuple-element.9.split_ref), custom_call_target="tpu_custom_call" | custom-call | tf_op jit(solution)/shard_map/gradient/pallas_call | solution.py:715

commit v5 on v4

--- a/solution.py
+++ b/solution.py
@@ -55,8 +55,10 @@
     table_hbm,
     idx_hbm,
     rank_hbm,
+    returns_hbm,
+    tt_hbm,
+    split_hbm,
     returns_ref,
-    tt_hbm,
     split_ref,
     leak_ref,
     bias_ref,
@@ -582,7 +584,9 @@
         pltpu.make_async_copy(tt_all.at[part], tt_hbm.at[part], local_sem.at[15 + i])
         for i, part in enumerate((core, 1 - core))
     ]
+    saves.append(pltpu.make_async_copy(returns_ref, returns_hbm, local_sem.at[17]))
     saves[0].start()
+    saves[2].start()
     arrived("mate2")
     saves[1].start()
     if pops > 1:
@@ -600,13 +604,19 @@
     mixed = mixed * jnp.sqrt(jnp.float32(12.0 / (32 * pops)))
     top = mixed.astype(BF16)
     split_ref[...] = jnp.concatenate([top, (mixed - top.astype(F32)).astype(BF16)], axis=1)
+    saves.append(pltpu.make_async_copy(split_ref, split_hbm, local_sem.at[18]))
+    saves[3].start()
+    finish()
     for save in saves:
         save.wait()
-    finish()
-
-
-def gradient(returns_in, tt_hbm, split_ref, returns_ref, grad_hbm, tt_v, grad_v, in_sems, out_sems):
+
+
+def gradient(
+    returns_in, tt_hbm, split_hbm, returns_hbm, grad_hbm, tt_v, split_v, grad_v, in_sems, out_sems
+):
     blocks = CHIPS // 4
+    split_load = pltpu.make_async_copy(split_hbm, split_v, in_sems.at[blocks])
+    split_load.start()
     loads = [
         pltpu.make_async_copy(
             tt_hbm.at[:, pl.ds(4 * q, 4)], tt_v.at[:, pl.ds(4 * q, 4)], in_sems.at[q]
@@ -615,13 +625,16 @@
     ]
     for load in loads:
         load.start()
-    returns_ref[...] = returns_in[...]
+    returns_copy = pltpu.make_async_copy(returns_in, returns_hbm, out_sems.at[blocks])
+    returns_copy.start()
+    split_load.wait()
+    split = split_v[...]
     stores = []
     for q in range(blocks):
         loads[q].wait()
         for k in range(2):
             block = tt_v[k, 4 * q : 4 * q + 4].reshape(4 * COLS, KTAB)
-            both_parts = dot(block, split_ref[...])
+            both_parts = dot(block, split)
             rows = (both_parts[:, 0:COLS] + both_parts[:, COLS:PAIR]).astype(BF16)
             for n in range(4):
                 start = PAIR * (4 * q + n) + COLS * k
@@ -629,7 +642,7 @@
         part = pl.ds(4 * PAIR * q, 4 * PAIR)
         stores.append(pltpu.make_async_copy(grad_v.at[part], grad_hbm.at[part], out_sems.at[q]))
         stores[-1].start()
-    for store in stores:
+    for store in stores + [returns_copy]:
         store.wait()
 
 
@@ -637,7 +650,6 @@
     in_spikes, w_in, w_rec, leak_rate, neuron_bias, readout, pert_table, pert_idx, member_ranks
 ):
     pops = lax.axis_size("pop")
-    vmem = pl.BlockSpec(memory_space=pltpu.VMEM)
     hbm = pl.BlockSpec(memory_space=pltpu.HBM)
     dma = pltpu.SemaphoreType.DMA
     returns, table_t, split = pl.pallas_call(
@@ -648,8 +660,10 @@
             jax.ShapeDtypeStruct((KTAB, PAIR), BF16),
         ),
         in_specs=[hbm] * 9,
-        out_specs=(vmem, hbm, vmem),
+        out_specs=(hbm, hbm, hbm),
         scratch_shapes=[
+            pltpu.VMEM((1, 32), F32),
+            pltpu.VMEM((KTAB, PAIR), BF16),
             pltpu.VMEM((1, COLS), F32),
             pltpu.VMEM((1, COLS), F32),
             pltpu.VMEM((1, COLS), F32),
@@ -677,7 +691,7 @@
             pltpu.VMEM((ROWS, PAIR), F32),
             pltpu.VMEM((CHIPS, ROWS, PAIR), BF16),
             pltpu.VMEM((128 * max(1, pops // 4), COLS), BF16),
-            dma((17,)),
+            dma((19,)),
             dma,
             dma,
             dma,
@@ -718,13 +732,14 @@
             jax.ShapeDtypeStruct((1, 32), F32),
             jax.ShapeDtypeStruct((NEUR, COLS), BF16),
         ),
-        in_specs=[vmem, hbm, vmem],
-        out_specs=(vmem, hbm),
+        in_specs=[hbm, hbm, hbm],
+        out_specs=(hbm, hbm),
         scratch_shapes=[
             pltpu.VMEM((2, CHIPS, COLS, KTAB), BF16),
+            pltpu.VMEM((KTAB, PAIR), BF16),
             pltpu.VMEM((NEUR, COLS), BF16),
-            dma((CHIPS // 4,)),
-            dma((CHIPS // 4,)),
+            dma((CHIPS // 4 + 1,)),
+            dma((CHIPS // 4 + 1,)),
         ],
         compiler_params=pltpu.CompilerParams(vmem_limit_bytes=60 * 1024 * 1024),
         name="gradient",

time: 66.9 us -> 64.9 us (0.970)
  Pallas kernels: 66 us -> 64.1 us
    pallas_call x1, Pallas kernels: 4.44 us -> 3.11 us  [shards(): pl.pallas_call(gradient, out_shape=(jax.ShapeDtypeStruct((1, 32), F32), j...]
where the time goes in v5:
time: 64.9 us; the launch traced here: 64.7 us
  Pallas kernels  64.1 us (99%)
    pallas_call x1, Pallas kernels, shards(): pl.pallas_call(functools.partial(kernel, pops), out_shape=(jax.ShapeDtype...  61 us
    pallas_call x1, Pallas kernels, shards(): pl.pallas_call(gradient, out_shape=(jax.ShapeDtypeStruct((1, 32), F32), j...  3.11 us

profile of v5, /device:TPU:1, one launch (start us, length us, event | category | flops | bytes accessed | tf_op | source)
XLA Modules:
  0.0 64.7 jit_solution(2127171886781821713)
XLA Ops:
  0.6 61.0 %rollout.1 = (f32[1,32]{1,0:T(1,128)}, bf16[2,16,128,256]{3,2,1,0:T(8,128)(2,1)}, bf16[256,256]{1,0:T(8,128)(2,1)}) custom-call(s32[15,4,4096]{2,1,0:T(4,128)} %bitcast.7, bf16[4096,128]{1,0:T(8,128)(2,1)} %w_in_hbm.1, bf16[4096,128]{1,0:T(8,128)(2,1)} %w_rec_hbm.1, f32[1,128]{1,0:T(1,128)} %bitcast.9, f32[1,128]{1,0:T(1,128)} %bitcast.10, ...), custom_call_target="tpu_custom_call" | custom-call | tf_op jit(solution)/shard_map/rollout/pallas_call | solution.py:655
  61.6 3.1 %gradient.1 = (f32[1,32]{1,0:T(1,128)}, bf16[4096,128]{1,0:T(8,128)(2,1)}) custom-call(f32[1,32]{1,0:T(1,128)} %get-tuple-element.7.returns_in, bf16[2,16,128,256]{3,2,1,0:T(8,128)(2,1)} %get-tuple-element.8.tt_hbm, bf16[256,256]{1,0:T(8,128)(2,1)} %get-tuple-element.9.split_hbm), custom_call_target="tpu_custom_call" | custom-call | tf_op jit(solution)/shard_map/gradient/pallas_call | solution.py:729

commit v6 on v5

--- a/solution.py
+++ b/solution.py
@@ -27,6 +27,7 @@
 LOW = 48
 NEUR = 4096
 KTAB = 256
+BLOCK = 2
 
 NT = (((1,), (1,)), ((), ()))
 TN = (((0,), (0,)), ((), ()))
@@ -201,36 +202,6 @@
                 device_id_type=MESH,
             ).start()
 
-    lane1 = lax.broadcasted_iota(jnp.int32, (1, 128), 1)
-    here = lax.div(lane1, 32) == lax.rem(pop, 4)
-
-    def placed(row):
-        return jnp.where(here, jnp.concatenate([row, row, row, row], axis=1), 0.0)
-
-    small[0].wait()
-    indices = idx_ref[...].astype(F32)
-    meta[pop, 0:1, :] = placed(indices[0:1])
-    meta[pop, 1:2, :] = placed(indices[1:2])
-    meta[pop, 2:8, :] = jnp.zeros((6, 128), F32)
-
-    loads[0].wait()
-    spot = lax.broadcasted_iota(jnp.int32, (32, KTAB), 1).astype(F32)
-    diagonal = lax.broadcasted_iota(jnp.int32, (32, 32), 0) == lax.broadcasted_iota(
-        jnp.int32, (32, 32), 1
-    )
-
-    def picks(row):
-        column = jnp.sum(jnp.where(diagonal, row, 0.0), axis=1, keepdims=True)
-        return jnp.where(spot == column, 1.0, 0.0).astype(BF16)
-
-    pick = jnp.concatenate([picks(indices[0:1]), picks(indices[1:2])], axis=0)
-    picked = dot(pick, table_v[...]).astype(BF16)
-    for half in range(2):
-        rows_src[half, 0:16, :] = picked[16 * half : 16 * half + 16]
-        rows_src[half, 16:32, :] = picked[32 + 16 * half : 48 + 16 * half]
-    rows_v[me] = rows_src[core]
-    tt_all[core, chip] = table_v[...].astype(F32).T.astype(BF16)
-
     for load in small[1:]:
         load.wait()
     drive = jnp.broadcast_to(bias_ref[...], (STEPS * EP, COLS))
@@ -248,18 +219,49 @@
 
     drive0 = drive_at(0)
     drive1 = drive_at(1)
+    spikes0 = squash(drive0)
+    m1[me] = spikes0
+
+    pl.semaphore_wait(barrier, TP - 1 + pops - 1)
+
+
+    push(m1.at[me], m1.at[me], plane, m1_send, m1_recv)
+    exchanged("m1", m1, TP - 1, m1_send, m1_recv)
+
+    lane1 = lax.broadcasted_iota(jnp.int32, (1, 128), 1)
+    here = lax.div(lane1, 32) == lax.rem(pop, 4)
+
+    def placed(row):
+        return jnp.where(here, jnp.concatenate([row, row, row, row], axis=1), 0.0)
+
+    small[0].wait()
+    indices = idx_ref[...].astype(F32)
+    meta[pop, 0:1, :] = placed(indices[0:1])
+    meta[pop, 1:2, :] = placed(indices[1:2])
+    meta[pop, 2:8, :] = jnp.zeros((6, 128), F32)
+
+    loads[0].wait()
+    spot = lax.broadcasted_iota(jnp.int32, (32, KTAB), 1).astype(F32)
+    diagonal = lax.broadcasted_iota(jnp.int32, (32, 32), 0) == lax.broadcasted_iota(
+        jnp.int32, (32, 32), 1
+    )
+
+    def picks(row):
+        column = jnp.sum(jnp.where(diagonal, row, 0.0), axis=1, keepdims=True)
+        return jnp.where(spot == column, 1.0, 0.0).astype(BF16)
+
+    pick = jnp.concatenate([picks(indices[0:1]), picks(indices[1:2])], axis=0)
+    picked = dot(pick, table_v[...]).astype(BF16)
+    for half in range(2):
+        rows_src[half, 0:16, :] = picked[16 * half : 16 * half + 16]
+        rows_src[half, 16:32, :] = picked[32 + 16 * half : 48 + 16 * half]
+    rows_v[me] = rows_src[core]
+    tt_all[core, chip] = table_v[...].astype(F32).T.astype(BF16)
+
     pair_v[core, 0:16, :] = drive_at(2)
     pair_v[core, 16:32, :] = drive_at(3)
     pair_v[core, 32:40, :] = jnp.broadcast_to(leak_ref[...], (8, 128))
     pair_v[core, 40:48, :] = jnp.broadcast_to(readout_ref[...], (8, 128))
-    spikes0 = squash(drive0)
-    m1[me] = spikes0
-
-    pl.semaphore_wait(barrier, TP - 1 + pops - 1)
-
-
-    push(m1.at[me], m1.at[me], plane, m1_send, m1_recv)
-    exchanged("m1", m1, TP - 1, m1_send, m1_recv)
     push(rows_src, rows_v.at[me], plane, rows_send, rows_recv, by_core=True)
     exchanged("rows", rows_v, TP - 1, rows_send, rows_recv)
 
@@ -614,12 +616,12 @@
 def gradient(
     returns_in, tt_hbm, split_hbm, returns_hbm, grad_hbm, tt_v, split_v, grad_v, in_sems, out_sems
 ):
-    blocks = CHIPS // 4
+    blocks = CHIPS // BLOCK
     split_load = pltpu.make_async_copy(split_hbm, split_v, in_sems.at[blocks])
     split_load.start()
     loads = [
         pltpu.make_async_copy(
-            tt_hbm.at[:, pl.ds(4 * q, 4)], tt_v.at[:, pl.ds(4 * q, 4)], in_sems.at[q]
+            tt_hbm.at[:, pl.ds(BLOCK * q, BLOCK)], tt_v.at[:, pl.ds(BLOCK * q, BLOCK)], in_sems.at[q]
         )
         for q in range(blocks)
     ]
@@ -633,13 +635,13 @@
     for q in range(blocks):
         loads[q].wait()
         for k in range(2):
-            block = tt_v[k, 4 * q : 4 * q + 4].reshape(4 * COLS, KTAB)
+            block = tt_v[k, BLOCK * q : BLOCK * (q + 1)].reshape(BLOCK * COLS, KTAB)
             both_parts = dot(block, split)
             rows = (both_parts[:, 0:COLS] + both_parts[:, COLS:PAIR]).astype(BF16)
-            for n in range(4):
-                start = PAIR * (4 * q + n) + COLS * k
+            for n in range(BLOCK):
+                start = PAIR * (BLOCK * q + n) + COLS * k
                 grad_v[start : start + COLS, :] = rows[COLS * n : COLS * (n + 1)]
-        part = pl.ds(4 * PAIR * q, 4 * PAIR)
+        part = pl.ds(BLOCK * PAIR * q, BLOCK * PAIR)
         stores.append(pltpu.make_async_copy(grad_v.at[part], grad_hbm.at[part], out_sems.at[q]))
         stores[-1].start()
     for store in stores + [returns_copy]:
@@ -738,8 +740,8 @@
             pltpu.VMEM((2, CHIPS, COLS, KTAB), BF16),
             pltpu.VMEM((KTAB, PAIR), BF16),
             pltpu.VMEM((NEUR, COLS), BF16),
-            dma((CHIPS // 4 + 1,)),
-            dma((CHIPS // 4 + 1,)),
+            dma((CHIPS // BLOCK + 1,)),
+            dma((CHIPS // BLOCK + 1,)),
         ],
         compiler_params=pltpu.CompilerParams(vmem_limit_bytes=60 * 1024 * 1024),
         name="gradient",

time: 64.9 us -> 65.4 us (level)
  no operation moved by 1% of the time
where the time goes in v6:
time: 65.4 us; the launch traced here: 65.2 us
  Pallas kernels  64.6 us (99%)
    pallas_call x1, Pallas kernels, shards(): pl.pallas_call(functools.partial(kernel, pops), out_shape=(jax.ShapeDtype...  60.9 us
    pallas_call x1, Pallas kernels, shards(): pl.pallas_call(gradient, out_shape=(jax.ShapeDtypeStruct((1, 32), F32), j...  3.68 us

profile of v6, /device:TPU:1, one launch (start us, length us, event | category | flops | bytes accessed | tf_op | source)
XLA Modules:
  0.0 65.2 jit_solution(15942241787652016597)
XLA Ops:
  0.6 60.9 %rollout.1 = (f32[1,32]{1,0:T(1,128)}, bf16[2,16,128,256]{3,2,1,0:T(8,128)(2,1)}, bf16[256,256]{1,0:T(8,128)(2,1)}) custom-call(s32[15,4,4096]{2,1,0:T(4,128)} %bitcast.7, bf16[4096,128]{1,0:T(8,128)(2,1)} %w_in_hbm.1, bf16[4096,128]{1,0:T(8,128)(2,1)} %w_rec_hbm.1, f32[1,128]{1,0:T(1,128)} %bitcast.9, f32[1,128]{1,0:T(1,128)} %bitcast.10, ...), custom_call_target="tpu_custom_call" | custom-call | tf_op jit(solution)/shard_map/rollout/pallas_call | solution.py:657
  61.5 3.7 %gradient.1 = (f32[1,32]{1,0:T(1,128)}, bf16[4096,128]{1,0:T(8,128)(2,1)}) custom-call(f32[1,32]{1,0:T(1,128)} %get-tuple-element.7.returns_in, bf16[2,16,128,256]{3,2,1,0:T(8,128)(2,1)} %get-tuple-element.8.tt_hbm, bf16[256,256]{1,0:T(8,128)(2,1)} %get-tuple-element.9.split_hbm), custom_call_target="tpu_custom_call" | custom-call | tf_op jit(solution)/shard_map/gradient/pallas_call | solution.py:731
